TPU v7x, 256 devices: a whole 4x4x8 slice. The times are simulated.
256 devices in a mesh: clus: 32 (over y, z), samp: 8 (over x, core).
Axes of the slice: x: 4, y: 4, z: 8, core: 2. Of those that a mesh axis runs over, the one named last changes fastest.
Arguments:
- currents: float32 [2048, 2, 128], P(('clus', 'samp')), may hold values from -6 to 6
- near_blocks: float32 [2048, 8, 2, 128, 128], P(('clus', 'samp')), may hold values from -0.125 to 0.125
- neighbours: int32 [2048, 8], P(('clus', 'samp')), may hold values from 0 to 2047, as said below
- near_count: int32 [2048], P(('clus', 'samp')), may hold values from 4 to 8
- radiation: float32 [2048, 2, 2, 128, 128], P(('clus', 'samp')), may hold values from -0.375 to 0.375
- interp_leaf: float32 [128, 256], replicated, may hold values from -0.1875 to 0.1875
- phase_leaf: float32 [8, 256], replicated, may hold values from -3.140625 to 3.140625
- interp_upper: float32 [256, 768], P(None, 'samp'), may hold values from -0.125 to 0.125
- phase_upper: float32 [8, 768], P(None, 'samp'), may hold values from -3.140625 to 3.140625
- tables_lower: float32 [64, 2, 256], replicated, may hold values from -1 to 1
- operator_lower: int32 [256, 16], replicated, may hold values from 0 to 63
- sources_lower: int32 [256, 16], replicated, may hold values from 0 to 255, as said below
- count_lower: int32 [256], replicated, may hold values from 8 to 16
- tables_upper: float32 [64, 2, 768], P(None, None, 'samp'), may hold values from -1.5 to 1.5
- operator_upper: int32 [32, 7], replicated, may hold values from 0 to 63
- sources_upper: int32 [32, 7], replicated, may hold values from 0 to 31, as said below
- count_upper: int32 [32], replicated, may hold values from 3 to 7
Outputs:
- near_field: float32 [2048, 2, 128], P(('clus', 'samp'))
- incoming_lower: float32 [256, 2, 2, 256], P(('clus', 'samp'))
- incoming_upper: float32 [32, 2, 2, 768], P('clus', None, None, 'samp')
Inputs may be any that keep to these rules, and one draw needn't show every extreme that they name: `neighbours`: the first slot of each leaf box is the box itself; every entry lies within 8 of its row's box index. `sources_lower`: the entries of a row are distinct and differ from the row's own box. `sources_upper`: the entries of a row are distinct and differ from the row's own box.
All inputs are finite; a program needn't handle non-finite values.
Results may differ from a plain program's by a relative error of at most 0.00007.
Values sent between devices are 32-bit elements; how exact they have to be, the bound alone decides.
No kernel may reach another device: no remote copies, remote signals or barrier semaphores. Data moves between devices by JAX's collectives and lax.ppermute only.
A program may use at most 64 MiB of HBM per device.

v0:
```python
import jax
import jax.numpy as jnp
from jax import lax
from jax.sharding import Mesh
from jax.sharding import PartitionSpec as P

CLUS_SAMP = ("clus_0", "clus_1", "samp_0", "samp_1")
SAMP = ("samp_0", "samp_1")
CLUS = ("clus_0", "clus_1")


highest = lax.Precision.HIGHEST


def extended(array, sides, width):
    edges = {}
    for axis, dim in sides:
        size, length = (lax.axis_size(axis), array.shape[dim])
        up = [(i, (i + 1) % size) for i in range(size - 1)]
        last = lax.slice_in_dim(array, length - width, length, axis=dim)
        leading = lax.slice_in_dim(array, 0, width, axis=dim)
        edges[dim] = (
            lax.ppermute(last, axis, up),
            lax.ppermute(leading, axis, [(b, a) for a, b in up]),
        )
    done = []
    for _, dim in sides:
        low, high = edges[dim]
        around = [(width, width) if d in done else (0, 0) for d in range(array.ndim)]
        array = jnp.concatenate([jnp.pad(low, around), array, jnp.pad(high, around)], axis=dim)
        done.append(dim)
    return array


def copy_for_each(array, axis):
    copies = jnp.broadcast_to(array, (lax.axis_size(axis), *array.shape))
    return lax.all_to_all(copies, axis, split_axis=0, concat_axis=0, tiled=True)


def in_order(blocks, dim):
    shape = list(blocks.shape[1:])
    shape[dim] *= blocks.shape[0]
    return jnp.moveaxis(blocks, 0, dim).reshape(shape)


def gathered_by_axis(array, axes, dim):
    far, near = axes
    blocks = copy_for_each(copy_for_each(array, far), near)
    return in_order(blocks.swapaxes(0, 1).reshape(-1, *array.shape), dim)


def collect(array, axis, dim):
    return in_order(copy_for_each(array, axis), dim)


def shift_children(values, phases):
    cosine = jnp.cos(phases)[None, :, None, :]
    sine_part = jnp.sin(phases)[None, :, None, :]
    real_part = values[:, :, :, 0]
    imag_part = values[:, :, :, 1]
    moved = jnp.stack(
        [cosine * real_part - sine_part * imag_part, sine_part * real_part + cosine * imag_part],
        axis=3,
    )
    return jnp.sum(moved, axis=1)


def rotate_rows(values, phases):
    cosine = jnp.cos(phases)[:, None, :]
    sine_part = jnp.sin(phases)[:, None, :]
    real_part = values[:, :, 0]
    imag_part = values[:, :, 1]
    return jnp.stack(
        [cosine * real_part - sine_part * imag_part, sine_part * real_part + cosine * imag_part],
        axis=2,
    )


def listed_weights(source_rows, operator_rows, count_rows, tables, box_total):
    slot_count = source_rows.shape[1]
    usable = (jnp.arange(slot_count)[None, :] < count_rows[:, None]).astype(jnp.float32)
    selected = tables[operator_rows]
    matches = (source_rows[:, :, None] == jnp.arange(box_total)[None, None, :]).astype(
        jnp.float32
    ) * usable[:, :, None]
    return jnp.einsum("rjq,rjck->rqck", matches, selected, precision=highest)


def fold_listed(coefficients, portion):
    c_real = coefficients[:, :, 0]
    c_imag = coefficients[:, :, 1]
    p_real = portion[:, :, 0]
    p_imag = portion[:, :, 1]
    out_real = jnp.einsum("rqk,qpk->rpk", c_real, p_real, precision=highest) - jnp.einsum(
        "rqk,qpk->rpk", c_imag, p_imag, precision=highest
    )
    out_imag = jnp.einsum("rqk,qpk->rpk", c_real, p_imag, precision=highest) + jnp.einsum(
        "rqk,qpk->rpk", c_imag, p_real, precision=highest
    )
    return jnp.stack([out_real, out_imag], axis=2)


def local(
    currents,
    near_blocks,
    neighbours,
    near_count,
    radiation,
    interp_leaf,
    phase_leaf,
    interp_upper,
    phase_upper,
    tables_lower,
    operator_lower,
    sources_lower,
    count_lower,
    tables_upper,
    operator_upper,
    sources_upper,
    count_upper,
):
    box_dev = currents.shape[0]
    slot_count = neighbours.shape[1]
    device_index = lax.axis_index(CLUS_SAMP)
    widened = extended(currents, ((CLUS_SAMP, 0),), box_dev)
    fetched = widened[neighbours - (device_index * box_dev - box_dev)]
    usable = (jnp.arange(slot_count)[None, :] < near_count[:, None]).astype(jnp.float32)
    fetched = fetched * usable[:, :, None, None]
    products = jnp.einsum("bkcij,bkdj->bcdi", near_blocks, fetched, precision=highest)
    near_field = jnp.stack(
        [products[:, 0, 0] - products[:, 1, 1], products[:, 0, 1] + products[:, 1, 0]], axis=1
    )
    radiated = jnp.einsum("bpcmk,bdm->bpcdk", radiation, currents, precision=highest)
    leaf_patterns = jnp.stack(
        [radiated[:, :, 0, 0] - radiated[:, :, 1, 1], radiated[:, :, 0, 1] + radiated[:, :, 1, 0]],
        axis=2,
    )
    interpolated = jnp.einsum("bpck,kt->bpct", leaf_patterns, interp_leaf, precision=highest)
    lower_dev = box_dev // 8
    samples_lower = interp_leaf.shape[1]
    lower_patterns = shift_children(
        interpolated.reshape(lower_dev, 8, 2, 2, samples_lower), phase_leaf
    )
    lower_total = lax.axis_size(CLUS_SAMP) * lower_dev
    first_lower = device_index * lower_dev
    coefficients = listed_weights(
        lax.dynamic_slice_in_dim(sources_lower, first_lower, lower_dev, 0),
        lax.dynamic_slice_in_dim(operator_lower, first_lower, lower_dev, 0),
        lax.dynamic_slice_in_dim(count_lower, first_lower, lower_dev, 0),
        tables_lower,
        lower_total,
    )
    incoming_lower = fold_listed(
        coefficients,
        gathered_by_axis(lower_patterns, (("clus_0", "clus_1"), ("samp_0", "samp_1")), 0),
    )
    lifted = jnp.einsum(
        "npck,ku->npcu", collect(lower_patterns, SAMP, 0), interp_upper, precision=highest
    )
    contributions = rotate_rows(lifted, phase_upper)
    upper_patterns = jnp.sum(contributions, axis=0, keepdims=True)
    clus_index = lax.axis_index(CLUS)
    upper_total = lax.axis_size(CLUS)
    coefficients_upper = listed_weights(
        lax.dynamic_slice_in_dim(sources_upper, clus_index, 1, 0),
        lax.dynamic_slice_in_dim(operator_upper, clus_index, 1, 0),
        lax.dynamic_slice_in_dim(count_upper, clus_index, 1, 0),
        tables_upper,
        upper_total,
    )
    incoming_upper = fold_listed(coefficients_upper, collect(upper_patterns, CLUS, 0))
    return (near_field, incoming_lower, incoming_upper)


def solution(mesh):
    split = Mesh(mesh.devices.reshape(4, 8, 4, 2), ("clus_0", "clus_1", "samp_0", "samp_1"))
    return jax.shard_map(
        local,
        mesh=split,
        in_specs=(
            P(CLUS_SAMP, None, None),
            P(CLUS_SAMP, None, None, None, None),
            P(CLUS_SAMP, None),
            P(CLUS_SAMP),
            P(CLUS_SAMP, None, None, None, None),
            P(),
            P(),
            P(None, SAMP),
            P(None, SAMP),
            P(),
            P(),
            P(),
            P(),
            P(None, None, SAMP),
            P(),
            P(),
            P(),
        ),
        out_specs=(
            P(CLUS_SAMP, None, None),
            P(CLUS_SAMP, None, None, None),
            P(CLUS, None, None, SAMP),
        ),
        check_vma=False,
    )
```

profile of v0, /device:TPU:1, one launch (start us, length us, event | category | flops | bytes accessed | tf_op | source)
XLA Modules:
  0.0 93.2 jit_solution(7244598334597756803)
XLA Ops:
  0.6 0.0 copy-start
  0.6 5.2 %collective-permute-start.1 = (f32[8,2,128]{2,1,0:T(2,128)}, f32[8,2,128]{2,1,0:T(2,128)S(1)}, u32[]{:S(2)}, u32[]{:S(2)}) collective-permute-start(f32[8,2,128]{2,1,0:T(2,128)} %param.17), channel_id=1, source_target_pairs={{1,0},{2,1},{3,2},{4,3},{5,4},{6,5},{7,6},{8,7},{9,8},{10,9},{11,1... | collective-permute-start | bytes 24584 | tf_op jit(solution)/shard_map/ppermute | solution.py:24
  5.9 1.9 %collective-permute-start = (f32[8,2,128]{2,1,0:T(2,128)}, f32[8,2,128]{2,1,0:T(2,128)S(1)}, u32[]{:S(2)}, u32[]{:S(2)}) collective-permute-start(f32[8,2,128]{2,1,0:T(2,128)} %param.17), channel_id=1, source_target_pairs={{0,1},{1,2},{2,3},{3,4},{4,5},{5,6},{6,7},{7,8},{8,9},{9,10},{10,1... | collective-permute-start | bytes 24584 | tf_op jit(solution)/shard_map/ppermute | solution.py:23
  7.8 0.0 copy-done
  7.8 1.8 %convolution_bitcast_fusion.3 = f32[8,2,2,2,128]{4,3,2,1,0:T(2,128)S(1)} fusion(f32[8,2,2,128,128]{4,3,2,1,0:T(8,128)S(1)} %copy-done, f32[8,2,128]{2,1,0:T(2,128)} %param.17), kind=kOutput, calls=%fused_computation.6 | convolution fusion | flops 12582912 | bytes 2138112 | tf_op jit(solution)/shard_map/bpcmk,bdm->bpcdk/dot_general | solution.py:133
  9.7 0.7 fusion.30
  10.5 1.1 %convolution_bitcast_fusion.2 = f32[1,8,2,2,256]{4,1,3,2,0:T(8,128)S(1)} fusion(f32[128,256]{1,0:T(8,128)} %param.22, f32[8,2,2,128]{3,1,0,2:T(2,128)S(1)} %pad_maximum_fusion.1), kind=kOutput, calls=%fused_computation.5 | convolution fusion | flops 12582912 | bytes 180224 | tf_op jit(solution)/shard_map/bpck,kt->bpct/dot_general | solution.py:138
  11.6 0.6 broadcast_in_dim.18
  12.2 5.6 %all-to-all-start.2 = ((f32[8,1,2,2,256]{4,3,2,1,0:T(2,128)}), f32[8,1,2,2,256]{4,3,2,1,0:T(2,128)S(1)}, u32[]{:S(2)}, u32[]{:S(2)}) async-start(f32[8,1,2,2,256]{4,3,2,1,0:T(2,128)} %broadcast_in_dim.18), calls=%async_computation.2 | async-start | bytes 65536 | tf_op jit(solution)/shard_map/all_to_all | solution.py:37
  17.8 0.7 compare_select_fusion.2
  18.5 0.1 reshape.374
  18.6 0.7 fusion.21
  19.3 0.9 fusion.12
  20.2 1.3 %dynamic_slice.24 = s32[1]{0:T(128)} dynamic-slice(s32[256]{0:T(256)} %param.29, s32[]{:T(128)S(6)} %select_n.20), dynamic_slice_sizes={1} | dynamic-slice | bytes 12 | tf_op jit(solution)/shard_map/dynamic_slice | solution.py:149
  21.5 0.6 compare_convert_fusion.1
  22.2 1.5 %gather_fusion.1 = f32[16,2,256]{2,1,0:T(2,128)S(1)} fusion(f32[64,2,256]{2,1,0:T(2,128)} %param.26, s32[1024]{0:T(1024)S(1)} %pad_clamp_fusion.1), kind=kCustom, calls=%fused_computation.1 | custom fusion | bytes 65600 | tf_op jit(solution)/shard_map/gather | solution.py:82
  23.7 0.7 convolution_bitcast_fusion
  24.4 0.8 slice_bitcast_fusion.3
  25.1 0.7 fusion.31
  25.8 0.9 fusion.18
  26.8 1.2 %dynamic_slice.28 = s32[1]{0:T(128)} dynamic-slice(s32[32]{0:T(128)} %param.33, s32[]{:T(128)S(6)} %select_n.22), dynamic_slice_sizes={1} | dynamic-slice | bytes 12 | tf_op jit(solution)/shard_map/dynamic_slice | solution.py:167
  28.0 0.6 compare_convert_fusion
  28.7 1.4 %gather_fusion.2 = f32[7,2,96]{2,1,0:T(2,128)S(1)} fusion(f32[64,2,96]{2,1,0:T(2,128)} %param.30, s32[1024]{0:T(1024)S(1)} %pad_clamp_fusion), kind=kCustom, calls=%fused_computation.2 | custom fusion | bytes 10780 | tf_op jit(solution)/shard_map/gather | solution.py:82
  30.1 0.3 convolution_bitcast_fusion.1
  30.4 0.0 collective-permute-done.1
  30.4 0.0 collective-permute-done
  30.4 0.7 pad_maximum_fusion
  31.2 0.7 gather_fusion
  31.8 0.0 all-to-all-done.2
  31.8 0.7 broadcast_in_dim.15
  32.5 12.0 %all-to-all-start = ((f32[32,1,2,2,256]{4,3,2,1,0:T(2,128)}), f32[32,1,2,2,256]{4,3,2,1,0:T(2,128)S(1)}, u32[]{:S(2)}, u32[]{:S(2)}) async-start(f32[32,1,2,2,256]{4,3,2,1,0:T(2,128)} %broadcast_in_dim.15), calls=%async_computation | async-start | bytes 262144 | tf_op jit(solution)/shard_map/all_to_all | solution.py:37
  44.5 1.1 %fusion.1 = f32[8,2,2,96]{3,0,2,1:T(8,128)S(1)} fusion(f32[256,96]{0,1:T(8,128)} %param.24, f32[8,1,2,2,256]{4,3,2,1,0:T(2,128)S(1)} %all-to-all-done.2), kind=kOutput, calls=%fused_computation.18 | convolution fusion | flops 9437184 | bytes 143360 | tf_op jit(solution)/shard_map/npck,ku->npcu/dot_general | solution.py:157
  45.6 8.0 %all-to-all-done = f32[32,1,2,2,256]{4,3,2,1,0:T(2,128)S(1)} async-done(((f32[32,1,2,2,256]{4,3,2,1,0:T(2,128)}), f32[32,1,2,2,256]{4,3,2,1,0:T(2,128)S(1)}, u32[]{:S(2)}, u32[]{:S(2)}) %all-to-all-start) | async-done | bytes 131104 | tf_op jit(solution)/shard_map/all_to_all | solution.py:37
  53.6 0.6 broadcast_in_dim.19
  54.3 4.6 %all-to-all-start.3 = ((f32[32,1,2,2,96]{4,3,2,1,0:T(2,128)}), f32[32,1,2,2,96]{4,3,2,1,0:T(2,128)S(1)}, u32[]{:S(2)}, u32[]{:S(2)}) async-start(f32[32,1,2,2,96]{4,3,2,1,0:T(2,128)} %broadcast_in_dim.19), calls=%async_computation.3 | async-start | bytes 131072 | tf_op jit(solution)/shard_map/all_to_all | solution.py:37
  58.8 9.3 %convolution_bitcast_fusion.4 = f32[8,2,2,128]{3,2,1,0:T(2,128)S(1)} fusion(f32[8,8,2,128,128]{4,3,2,1,0:T(8,128)} %param.18, f32[8,8,2,128]{3,2,1,0:T(2,128)S(1)} %bitcast.148, f32[8,8]{1,0:T(8,128)S(1)} %fusion.21), kind=kOutput, calls=%fused_computation.7 | convolution fusion | flops 50348032 | bytes 8470784 | tf_op jit(solution)/shard_map/bkcij,bkdj->bcdi/dot_general | solution.py:129
  68.1 0.0 all-to-all-done.3
  68.2 1.1 %broadcast_in_dim.16 = f32[8,32,1,2,2,256]{5,1,4,3,2,0:T(8,128)} broadcast(f32[32,2,2,256]{3,0,2,1:T(8,128)S(1)} %copy.44), dimensions={1,3,4,5} | broadcast | bytes 1179648 | tf_op jit(solution)/shard_map/broadcast_in_dim | solution.py:36
  69.3 6.6 %all-to-all-start.1 = ((f32[8,32,1,2,2,256]{5,1,4,3,2,0:T(8,128)}), f32[8,32,1,2,2,256]{5,1,4,3,2,0:T(8,128)S(1)}, u32[]{:S(2)}, u32[]{:S(2)}) async-start(f32[8,32,1,2,2,256]{5,1,4,3,2,0:T(8,128)} %broadcast_in_dim.16), calls=%async_computation.1 | async-start | bytes 2097152 | tf_op jit(solution)/shard_map/all_to_all | solution.py:37
  75.9 0.6 copy.49
  76.5 0.1 fusion.27
  76.5 0.1 multiply_reduce_fusion.7
  76.6 0.6 pad_maximum_fusion.4
  77.2 13.6 %all-to-all-done.1 = f32[8,32,1,2,2,256]{5,1,4,3,2,0:T(8,128)S(1)} async-done(((f32[8,32,1,2,2,256]{5,1,4,3,2,0:T(8,128)}), f32[8,32,1,2,2,256]{5,1,4,3,2,0:T(8,128)S(1)}, u32[]{:S(2)}, u32[]{:S(2)}) %all-to-all-start.1) | async-done | bytes 1048608 | tf_op jit(solution)/shard_map/all_to_all | solution.py:37
  90.8 0.6 copy.122
  91.4 1.1 %multiply_reduce_fusion.2 = (f32[256,2]{0,1:T(2,128)S(1)}, f32[256,2]{0,1:T(2,128)S(1)}, f32[256,2]{0,1:T(2,128)S(1)}, f32[256,2]{0,1:T(2,128)S(1)}) fusion(f32[256,2,2,256]{3,0,2,1:T(8,128)S(1)} %bitcast.146, f32[256,256]{0,1:T(8,128)} %get-tuple-element.25, f32[256,256]{0,1:T(8,128)S(1)} %get-tuple-element.24), kind=kLoop, calls=%fused_computation.13 | loop fusion | flops 1046528 | bytes 1581056 | tf_op jit(solution)/shard_map/rqk,qpk->rpk/dot_general | solution.py:94
  92.6 0.6 pad_maximum_fusion.3
  (21 shorter events, 0.2 us)
Async XLA Ops:
  0.6 7.2 %copy-start = (f32[8,2,2,128,128]{4,3,2,1,0:T(8,128)S(1)}, f32[8,2,2,128,128]{4,3,2,1,0:T(8,128)}, u32[]{:S(2)}) copy-start(f32[8,2,2,128,128]{4,3,2,1,0:T(8,128)} %param.21) | copy-start | bytes 6291460
  0.6 29.8 %collective-permute-start.1 = (f32[8,2,128]{2,1,0:T(2,128)}, f32[8,2,128]{2,1,0:T(2,128)S(1)}, u32[]{:S(2)}, u32[]{:S(2)}) collective-permute-start(f32[8,2,128]{2,1,0:T(2,128)} %param.17), channel_id=1, source_target_pairs={{1,0},{2,1},{3,2},{4,3},{5,4},{6,5},{7,6},{8,7},{9,8},{10,9},{11,1... | collective-permute-start | bytes 24584 | tf_op jit(solution)/shard_map/ppermute | solution.py:24
  5.9 24.5 %collective-permute-start = (f32[8,2,128]{2,1,0:T(2,128)}, f32[8,2,128]{2,1,0:T(2,128)S(1)}, u32[]{:S(2)}, u32[]{:S(2)}) collective-permute-start(f32[8,2,128]{2,1,0:T(2,128)} %param.17), channel_id=1, source_target_pairs={{0,1},{1,2},{2,3},{3,4},{4,5},{5,6},{6,7},{7,8},{8,9},{9,10},{10,1... | collective-permute-start | bytes 24584 | tf_op jit(solution)/shard_map/ppermute | solution.py:23
  12.2 19.6 %all-to-all-start.2 = ((f32[8,1,2,2,256]{4,3,2,1,0:T(2,128)}), f32[8,1,2,2,256]{4,3,2,1,0:T(2,128)S(1)}, u32[]{:S(2)}, u32[]{:S(2)}) async-start(f32[8,1,2,2,256]{4,3,2,1,0:T(2,128)} %broadcast_in_dim.18), calls=%async_computation.2 | async-start | bytes 65536 | tf_op jit(solution)/shard_map/all_to_all | solution.py:37
  32.5 21.1 %all-to-all-start = ((f32[32,1,2,2,256]{4,3,2,1,0:T(2,128)}), f32[32,1,2,2,256]{4,3,2,1,0:T(2,128)S(1)}, u32[]{:S(2)}, u32[]{:S(2)}) async-start(f32[32,1,2,2,256]{4,3,2,1,0:T(2,128)} %broadcast_in_dim.15), calls=%async_computation | async-start | bytes 262144 | tf_op jit(solution)/shard_map/all_to_all | solution.py:37
  54.3 13.9 %all-to-all-start.3 = ((f32[32,1,2,2,96]{4,3,2,1,0:T(2,128)}), f32[32,1,2,2,96]{4,3,2,1,0:T(2,128)S(1)}, u32[]{:S(2)}, u32[]{:S(2)}) async-start(f32[32,1,2,2,96]{4,3,2,1,0:T(2,128)} %broadcast_in_dim.19), calls=%async_computation.3 | async-start | bytes 131072 | tf_op jit(solution)/shard_map/all_to_all | solution.py:37
  69.3 21.5 %all-to-all-start.1 = ((f32[8,32,1,2,2,256]{5,1,4,3,2,0:T(8,128)}), f32[8,32,1,2,2,256]{5,1,4,3,2,0:T(8,128)S(1)}, u32[]{:S(2)}, u32[]{:S(2)}) async-start(f32[8,32,1,2,2,256]{5,1,4,3,2,0:T(8,128)} %broadcast_in_dim.16), calls=%async_computation.1 | async-start | bytes 2097152 | tf_op jit(solution)/shard_map/all_to_all | solution.py:37
where the time goes:
time: 94 us; the launch traced here: 93.2 us
  starting transfers between devices  35.9 us (38%)
  waiting for transfers between devices  21.6 us (23%)
  matrix products  14.3 us (15%)
  local copies, waits for them, and re-layouts  12.7 us (14%)
  other arithmetic  7.78 us (8%)
    all_to_all x4, starting transfers between devices, copy_for_each(): return lax.all_to_all(copies, axis, split_axis=0, concat_axis=0, tiled=True)  28.7 us
    all_to_all x4, waiting for transfers between devices, copy_for_each(): return lax.all_to_all(copies, axis, split_axis=0, concat_axis=0, tiled=True)  21.6 us
    dot_general x1, matrix products, local(): jnp.einsum('bkcij,bkdj->bcdi', near_blocks, fetched, precision=highest)  9.25 us
    ppermute x1, starting transfers between devices, extended(): lax.ppermute(leading, axis, [(b, a) for a, b in up])  5.24 us
    broadcast_in_dim x4, local copies, waits for them, and re-layouts, copy_for_each(): copies = jnp.broadcast_to(array, (lax.axis_size(axis), *array.shape))  3.03 us
    gather x2, local copies, waits for them, and re-layouts, listed_weights(): selected = tables[operator_rows]  2.91 us
    ppermute x1, starting transfers between devices, extended(): lax.ppermute(last, axis, up)  1.92 us
  transfers between devices with their start and end apart: 6, of which 2 were waited for; matrix products, arithmetic and copies ran while one was open for 32% of the time, Pallas kernels for 0%

commit v1 on v0

v1 whole, which is shorter than its diff:
```python
import functools

import jax
import jax.numpy as jnp
from jax import lax
from jax.experimental import pallas as pl
from jax.experimental.pallas import tpu as pltpu
from jax.sharding import Mesh
from jax.sharding import PartitionSpec as P

CLUS = ("clus_0", "clus_1")
SAMP = ("samp_0", "samp_1")
CLUS_SAMP = CLUS + SAMP

HIGHEST = lax.Precision.HIGHEST
F32 = jnp.float32
VMEM = pl.BlockSpec(memory_space=pltpu.VMEM)
SMEM = pl.BlockSpec(memory_space=pltpu.SMEM)
HBM = pl.BlockSpec(memory_space=pltpu.HBM)


def place():
    clus = lax.axis_index("clus_0") * 8 + lax.axis_index("clus_1")
    samp = lax.axis_index("samp_0") * 2 + lax.axis_index("samp_1")
    return clus, samp


def call(kernel, outs, in_specs, scratch=(), mib=16, flops=0, bytes_accessed=0, name=None):
    many = isinstance(outs, (list, tuple))
    run = pl.pallas_call(
        kernel,
        out_shape=outs,
        in_specs=in_specs,
        out_specs=[VMEM] * len(outs) if many else VMEM,
        scratch_shapes=list(scratch),
        compiler_params=pltpu.CompilerParams(vmem_limit_bytes=mib << 20),
        cost_estimate=pl.CostEstimate(flops=flops, bytes_accessed=bytes_accessed, transcendentals=0),
        name=name,
    )

    def placed(*operands):
        return run(
            *(
                pltpu.with_memory_space_constraint(x, pltpu.HBM) if spec is HBM else x
                for x, spec in zip(operands, in_specs)
            )
        )

    return placed


def rows_of(shape, axis):
    return lax.broadcasted_iota(jnp.int32, shape, axis)


def start_all(pairs, sems):
    copies = [pltpu.make_async_copy(a, b, sems.at[i]) for i, (a, b) in enumerate(pairs)]
    for copy in copies:
        copy.start()
    return copies


def leaf_kernel(cur_h, rad_h, interp_h, phase_h, out, cur, rad, interp, phase, pat, msg, sems):
    pairs = [(cur_h, cur)] + [(rad_h.at[b], rad.at[b]) for b in range(8)] + [(interp_h, interp), (phase_h, phase)]
    copies = start_all(pairs, sems)
    copies[0].wait()
    columns = cur[...].reshape(16, 128).T
    for b in range(8):
        copies[1 + b].wait()
        cr = jnp.broadcast_to(columns[:, 2 * b : 2 * b + 1], (128, 128))
        ci = jnp.broadcast_to(columns[:, 2 * b + 1 : 2 * b + 2], (128, 128))
        for p in range(2):
            rr = rad[b, p, 0]
            ri = rad[b, p, 1]
            pat[pl.ds(16 * p + b, 1), :] = jnp.sum(rr * cr - ri * ci, axis=0, keepdims=True)
            pat[pl.ds(16 * p + 8 + b, 1), :] = jnp.sum(rr * ci + ri * cr, axis=0, keepdims=True)
    copies[9].wait()
    copies[10].wait()
    lifted = jnp.dot(pat[...], interp[...], precision=HIGHEST, preferred_element_type=F32)
    cosine = jnp.cos(phase[...])
    sine = jnp.sin(phase[...])
    for p in range(2):
        yr = lifted[16 * p : 16 * p + 8]
        yi = lifted[16 * p + 8 : 16 * p + 16]
        re = jnp.sum(cosine * yr - sine * yi, axis=0, keepdims=True)
        im = jnp.sum(sine * yr + cosine * yi, axis=0, keepdims=True)
        for c, part in enumerate((re, im)):
            for h in range(2):
                msg[pl.ds(4 * p + 2 * c + h, 1), :] = part[:, 128 * h : 128 * h + 128]
    whole = msg[...]
    for peer in range(8):
        out[peer] = whole


def prep_kernel(
    src_low_h, op_low_h, cnt_low_h, src_up_h, op_up_h, cnt_up_h, tab_low_h, tab_up_h, phase_h, interp_h,
    wa, wb, ua, ub, rot, interp,
    src_low, op_low, cnt_low, src_up, op_up, cnt_up, tab_low, tab_up, phase, code_v, code_s, sem, sems,
):
    clus, samp = place()
    copies = start_all(
        [
            (src_low_h, src_low), (op_low_h, op_low), (cnt_low_h, cnt_low), (src_up_h, src_up),
            (op_up_h, op_up), (cnt_up_h, cnt_up), (phase_h, phase), (tab_low_h, tab_low),
            (tab_up_h, tab_up), (interp_h, interp),
        ],
        sems,
    )
    for copy in copies:
        copy.wait()
    src = src_low[...]
    used = (rows_of(src.shape, 0) < cnt_low[...]) & ((src >> 3) == clus)
    code = op_low[...] + 1
    octant = src & 7
    for o in range(8):
        code_v[pl.ds(o, 1), :] = jnp.sum(jnp.where(used & (octant == o), code, 0), axis=0, keepdims=True)
    code_v[pl.ds(8, 8), :] = jnp.zeros((8, 256), jnp.int32)
    used_up = (rows_of(src_up.shape, 0) < cnt_up[...]) & (src_up[...] == clus)
    code_v[pl.ds(8, 1), pl.ds(0, 32)] = jnp.sum(jnp.where(used_up, op_up[...] + 1, 0), axis=0, keepdims=True)
    copy = pltpu.make_async_copy(code_v, code_s, sem)
    copy.start()
    zero = jnp.zeros((8, 128), F32)
    row = rows_of((8, 128), 0)
    first_half = (row & 1) == 0
    sign_low = jnp.where((row & 2) == 0, -1.0, 1.0).astype(F32)
    sign_up = jnp.where((row & 1) == 0, -1.0, 1.0).astype(F32)[:, :96]
    rot[0] = zero
    rot[1] = zero
    rot[0, :, pl.ds(0, 96)] = jnp.cos(phase[...])
    rot[1, :, pl.ds(0, 96)] = jnp.sin(phase[...])
    copy.wait()

    def target(t, carry):
        for o in range(8):
            i = code_s[o, t * 8 + samp]
            n = jnp.maximum(i - 1, 0)
            listed = jnp.where(i > 0, 1.0, 0.0).astype(F32)
            parts = []
            for c in range(2):
                low = jnp.broadcast_to(tab_low[n, pl.ds(c, 1), pl.ds(0, 128)], (8, 128))
                high = jnp.broadcast_to(tab_low[n, pl.ds(c, 1), pl.ds(128, 128)], (8, 128))
                parts.append(jnp.where(first_half, low, high) * listed)
            wa[t, o] = parts[0]
            wb[t, o] = parts[1] * sign_low
        i = code_s[8, t]
        n = jnp.maximum(i - 1, 0)
        listed = jnp.where(i > 0, 1.0, 0.0).astype(F32)
        ua[t] = zero
        ub[t] = zero
        ua[t, :, pl.ds(0, 96)] = jnp.broadcast_to(tab_up[n, pl.ds(0, 1), :], (8, 96)) * listed
        ub[t, :, pl.ds(0, 96)] = jnp.broadcast_to(tab_up[n, pl.ds(1, 1), :], (8, 96)) * listed * sign_up
        return carry

    lax.fori_loop(0, 32, target, 0)


def middle_kernel(got, interp, wa, wb, ua, ub, rot, out, upper):
    row = rows_of((8, 128), 0)
    halves = []
    for h in range(2):
        halves.append(
            jnp.concatenate([got[pl.ds(2 * k + h, 8, stride=8), :] for k in range(4)], axis=0)
        )
    lifted = lax.dot_general(
        jnp.concatenate(halves, axis=1), interp[...], (((1,), (1,)), ((), ())),
        precision=HIGHEST, preferred_element_type=F32,
    )
    plain = [got[pl.ds(8 * o, 8), :] for o in range(8)]
    swapped = [
        jnp.where((row & 2) == 0, pltpu.roll(x, 6, 0), pltpu.roll(x, 2, 0)) for x in plain
    ]
    for t in range(32):
        total = wa[t, 0] * plain[0] + wb[t, 0] * swapped[0]
        for o in range(1, 8):
            total += wa[t, o] * plain[o] + wb[t, o] * swapped[o]
        out[t, pl.ds(0, 8), :] = total
    upper[...] = jnp.zeros((8, 128), F32)
    cosine = rot[0][:, :96]
    sine = rot[1][:, :96]
    for p in range(2):
        zr = lifted[16 * p : 16 * p + 8]
        zi = lifted[16 * p + 8 : 16 * p + 16]
        upper[pl.ds(2 * p, 1), pl.ds(0, 96)] = jnp.sum(cosine * zr - sine * zi, axis=0, keepdims=True)
        upper[pl.ds(2 * p + 1, 1), pl.ds(0, 96)] = jnp.sum(sine * zr + cosine * zi, axis=0, keepdims=True)
    up = upper[...]
    up_swapped = jnp.where((row & 1) == 0, pltpu.roll(up, 7, 0), pltpu.roll(up, 1, 0))
    for t in range(32):
        out[t, pl.ds(8, 8), :] = ua[t] * up + ub[t] * up_swapped


def near_kernel(cur, low, high, neighbours_h, count_h, blocks, out, held, ext, acc, neighbours, count, sems):
    clus, samp = place()
    base = (clus * 8 + samp) * 8 - 8

    def copy(b):
        return pltpu.make_async_copy(blocks.at[b], held.at[b], sems.at[b])

    for b in range(8):
        copy(b).start()
    lists = [
        pltpu.make_async_copy(cur, ext.at[pl.ds(8, 8)], sems.at[8]),
        pltpu.make_async_copy(neighbours_h, neighbours, sems.at[9]),
        pltpu.make_async_copy(count_h, count, sems.at[10]),
    ]
    for one in lists:
        one.start()
    ext[pl.ds(0, 8)] = low[...]
    ext[pl.ds(16, 8)] = high[...]
    for one in lists:
        one.wait()
    ones = jnp.ones((8, 128), F32)

    def box(b, carry):
        xs = []
        for k in range(8):
            i = neighbours[b, k] - base
            keep = jnp.where(k < count[b], 1.0, 0.0).astype(F32)
            xr = jnp.broadcast_to(ext[i, pl.ds(0, 1), :], (8, 128)) * keep
            xi = jnp.broadcast_to(ext[i, pl.ds(1, 1), :], (8, 128)) * keep
            xs.append((xr, xi))
        copy(b).wait()
        for it in range(16):
            re = None
            for k, (xr, xi) in enumerate(xs):
                br = held[b, k, 0, pl.ds(8 * it, 8), :]
                bi = held[b, k, 1, pl.ds(8 * it, 8), :]
                tr = br * xr - bi * xi
                ti = br * xi + bi * xr
                re, im = (tr, ti) if re is None else (re + tr, im + ti)
            acc[0, pl.ds(8 * it, 8), :] = re
            acc[1, pl.ds(8 * it, 8), :] = im
        for c in range(2):
            summed = lax.dot_general(
                ones, acc[c], (((1,), (1,)), ((), ())), precision=HIGHEST, preferred_element_type=F32
            )
            out[b, pl.ds(c, 1), :] = summed[0:1]
        return carry

    lax.fori_loop(0, 8, box, 0)


def final_kernel(got, out_low, out_up):
    low = got[0, pl.ds(0, 8), :]
    up = got[0, pl.ds(8, 8), :]
    for t in range(1, 32):
        low += got[t, pl.ds(0, 8), :]
        up += got[t, pl.ds(8, 8), :]
    for p in range(2):
        for c in range(2):
            k = 2 * p + c
            for h in range(2):
                out_low[0, p, pl.ds(c, 1), pl.ds(128 * h, 128)] = low[2 * k + h : 2 * k + h + 1]
            out_up[0, p, pl.ds(c, 1), :] = up[k : k + 1, :96]


def shape(*dims):
    return jax.ShapeDtypeStruct(dims, F32)


def local(
    currents, near_blocks, neighbours, near_count, radiation, interp_leaf, phase_leaf,
    interp_upper, phase_upper, tables_lower, operator_lower, sources_lower, count_lower,
    tables_upper, operator_upper, sources_upper, count_upper,
):
    message = call(
        leaf_kernel, shape(8, 8, 128), [HBM] * 4,
        [
            pltpu.VMEM((8, 2, 128), F32), pltpu.VMEM((8, 2, 2, 128, 128), F32),
            pltpu.VMEM((128, 256), F32), pltpu.VMEM((8, 256), F32),
            pltpu.VMEM((32, 128), F32), pltpu.VMEM((8, 128), F32), pltpu.SemaphoreType.DMA((11,)),
        ],
        flops=4 << 20, bytes_accessed=2 << 20, name="leaf",
    )(currents, radiation, interp_leaf, phase_leaf)
    own, message = lax.optimization_barrier((currents, message))
    gathered = lax.all_to_all(message, SAMP, split_axis=0, concat_axis=0, tiled=True)

    size = lax.axis_size(CLUS_SAMP)
    up = [(i, i + 1) for i in range(size - 1)]
    down = [(b, a) for a, b in up]
    low = lax.ppermute(own, CLUS_SAMP, up)
    high = lax.ppermute(own, CLUS_SAMP, down)

    wa, wb, ua, ub, rot, interp = call(
        prep_kernel,
        [
            shape(32, 8, 8, 128), shape(32, 8, 8, 128), shape(32, 8, 128), shape(32, 8, 128),
            shape(2, 8, 128), shape(96, 256),
        ],
        [HBM] * 10,
        [
            pltpu.VMEM((16, 256), jnp.int32), pltpu.VMEM((16, 256), jnp.int32), pltpu.VMEM((1, 256), jnp.int32),
            pltpu.VMEM((7, 32), jnp.int32), pltpu.VMEM((7, 32), jnp.int32), pltpu.VMEM((1, 32), jnp.int32),
            pltpu.VMEM((64, 2, 256), F32), pltpu.VMEM((64, 2, 96), F32), pltpu.VMEM((8, 96), F32),
            pltpu.VMEM((16, 256), jnp.int32), pltpu.SMEM((16, 256), jnp.int32), pltpu.SemaphoreType.DMA,
            pltpu.SemaphoreType.DMA((10,)),
        ],
        flops=1 << 20, bytes_accessed=4 << 20, name="prep",
    )(
        sources_lower.T, operator_lower.T, count_lower.reshape(1, -1),
        sources_upper.T, operator_upper.T, count_upper.reshape(1, -1),
        tables_lower, tables_upper, phase_upper, interp_upper.T,
    )

    payload = call(
        middle_kernel, shape(32, 16, 128), [VMEM] * 7, [pltpu.VMEM((8, 128), F32)],
        flops=4 << 20, bytes_accessed=3 << 20, name="middle",
    )(gathered.reshape(64, 128), interp, wa, wb, ua, ub, rot)
    parts = lax.all_to_all(payload, CLUS, split_axis=0, concat_axis=0, tiled=True)

    near_field = call(
        near_kernel, shape(8, 2, 128), [HBM, VMEM, VMEM, HBM, HBM, HBM],
        [
            pltpu.VMEM((8, 8, 2, 128, 128), F32),
            pltpu.VMEM((24, 2, 128), F32),
            pltpu.VMEM((2, 128, 128), F32),
            pltpu.SMEM((8, 8), jnp.int32),
            pltpu.SMEM((8,), jnp.int32),
            pltpu.SemaphoreType.DMA((11,)),
        ],
        flops=16 << 20, bytes_accessed=8 << 20, name="near",
    )(currents, low, high, neighbours, near_count, near_blocks)

    incoming_lower, incoming_upper = call(
        final_kernel, [shape(1, 2, 2, 256), shape(1, 2, 2, 96)], [VMEM],
        flops=1 << 17, bytes_accessed=1 << 18, name="final",
    )(parts)
    return near_field, incoming_lower, incoming_upper


def solution(mesh):
    split = Mesh(mesh.devices.reshape(4, 8, 4, 2), CLUS_SAMP)
    whole = P()
    return jax.shard_map(
        local,
        mesh=split,
        in_specs=(
            P(CLUS_SAMP), P(CLUS_SAMP), P(CLUS_SAMP), P(CLUS_SAMP), P(CLUS_SAMP),
            whole, whole, P(None, SAMP), P(None, SAMP),
            whole, whole, whole, whole, P(None, None, SAMP), whole, whole, whole,
        ),
        out_specs=(P(CLUS_SAMP), P(CLUS_SAMP), P(CLUS, None, None, SAMP)),
        check_vma=False,
    )
```

time: 94 us -> 46.6 us (0.50)
  the two profiles are of different devices: /device:TPU:1 before, /device:TPU:103 now
where the time goes in v1:
time: 46.6 us; the launch traced here: 46.2 us
  starting transfers between devices  23.7 us (51%)
  Pallas kernels  15.2 us (33%)
  waiting for transfers between devices  6.57 us (14%)
  between operations  0.7 us (2%)
    pallas_call x5, Pallas kernels, placed(): run(*(pltpu.with_memory_space_constraint(x, pltpu.HBM) if spec is HBM els...  15.2 us
    all_to_all x1, starting transfers between devices, local(): lax.all_to_all(payload, CLUS, split_axis=0, concat_axis=0, tiled=True)  9.89 us
    ppermute x1, starting transfers between devices, local(): low = lax.ppermute(own, CLUS_SAMP, up)  6.79 us
    ppermute x1, waiting for transfers between devices, local(): high = lax.ppermute(own, CLUS_SAMP, down)  6.56 us
    all_to_all x1, starting transfers between devices, local(): lax.all_to_all(message, SAMP, split_axis=0, concat_axis=0, tiled=True)  5.07 us
    ppermute x1, starting transfers between devices, local(): high = lax.ppermute(own, CLUS_SAMP, down)  1.92 us
  transfers between devices with their start and end apart: 4, of which 1 were waited for; matrix products, arithmetic and copies ran while one was open for 0% of the time, Pallas kernels for 23%

profile of v1, /device:TPU:103, one launch (start us, length us, event | category | flops | bytes accessed | tf_op | source)
XLA Modules:
  0.0 46.2 jit_solution(11244891359586442599)
XLA Ops:
  0.6 2.8 %leaf.1 = f32[8,8,128]{2,1,0:T(8,128)} custom-call(f32[8,2,128]{2,1,0:T(2,128)} %cur.1, f32[8,2,2,128,128]{4,3,2,1,0:T(8,128)} %rad_h.1, f32[128,256]{1,0:T(8,128)} %interp_h.1, f32[8,256]{1,0:T(8,128)} %phase_h.2), custom_call_target="tpu_custom_call" | custom-call | flops 4194304 | bytes 2097152 | tf_op jit(solution)/shard_map/leaf/pallas_call | solution.py:42
  3.4 5.1 %all-to-all-start = ((f32[8,8,128]{2,1,0:T(8,128)}), f32[8,8,128]{2,1,0:T(8,128)S(1)}, u32[]{:S(2)}, u32[]{:S(2)}) async-start(f32[8,8,128]{2,1,0:T(8,128)} %leaf.1), calls=%async_computation | async-start | bytes 65536 | tf_op jit(solution)/shard_map/all_to_all | solution.py:275
  8.5 3.2 %prep.1 = (f32[32,8,8,128]{3,2,1,0:T(8,128)S(1)}, f32[32,8,8,128]{3,2,1,0:T(8,128)S(1)}, f32[32,8,128]{2,1,0:T(8,128)S(1)}, f32[32,8,128]{2,1,0:T(8,128)S(1)}, f...) custom-call(s32[16,256]{1,0:T(8,128)} %bitcast.10, s32[16,256]{1,0:T(8,128)} %bitcast.11, s32[1,256]{1,0:T(1,128)} %bitcast.14, ...), custom_call_target="tpu_custom_call" | custom-call | flops 1048576 | bytes 4194304 | tf_op jit(solution)/shard_map/prep/pallas_call | solution.py:42
  11.7 0.0 all-to-all-done
  11.7 1.0 %middle.1 = f32[32,16,128]{2,1,0:T(8,128)} custom-call(f32[64,128]{1,0:T(8,128)S(1)} %bitcast.8, f32[96,256]{1,0:T(8,128)S(1)} %get-tuple-element.15.interp, f32[32,8,8,128]{3,2,1,0:T(8,128)S(1)} %get-tuple-element.16.wa, f32[32,8,8,128]{3,2,1,0:T(8,128)S(1)} %get-tuple-element.17.wb, f32[32,8,128]{2,1,0:T(8,128)S(1)} %get-tuple-element.18.ua, ...), custom_call_target="tpu_custom_call" | custom-call | flops 4194304 | bytes 3145728 | tf_op jit(solution)/shard_map/middle/pallas_call | solution.py:42
  12.7 9.9 %all-to-all-start.1 = ((f32[32,16,128]{2,1,0:T(8,128)}), f32[32,16,128]{2,1,0:T(8,128)S(1)}, u32[]{:S(2)}, u32[]{:S(2)}) async-start(f32[32,16,128]{2,1,0:T(8,128)} %middle.1), calls=%async_computation.1 | async-start | bytes 524288 | tf_op jit(solution)/shard_map/all_to_all | solution.py:308
  22.6 6.8 %collective-permute-start = (f32[8,2,128]{2,1,0:T(2,128)}, f32[8,2,128]{2,1,0:T(2,128)S(1)}, u32[]{:S(2)}, u32[]{:S(2)}) collective-permute-start(f32[8,2,128]{2,1,0:T(2,128)} %cur.1), channel_id=1, source_target_pairs={{0,1},{1,2},{2,3},{3,4},{4,5},{5,6},{6,7},{7,8},{8,9},{9,10},{10,1... | collective-permute-start | bytes 24584 | tf_op jit(solution)/shard_map/ppermute | solution.py:280
  29.4 1.9 %collective-permute-start.1 = (f32[8,2,128]{2,1,0:T(2,128)}, f32[8,2,128]{2,1,0:T(2,128)S(1)}, u32[]{:S(2)}, u32[]{:S(2)}) collective-permute-start(f32[8,2,128]{2,1,0:T(2,128)} %cur.1), channel_id=1, source_target_pairs={{1,0},{2,1},{3,2},{4,3},{5,4},{6,5},{7,6},{8,7},{9,8},{10,9},{11,1... | collective-permute-start | bytes 24584 | tf_op jit(solution)/shard_map/ppermute | solution.py:281
  31.3 0.0 collective-permute-done.low
  31.4 6.6 %collective-permute-done.1.high = f32[8,2,128]{2,1,0:T(2,128)S(1)} collective-permute-done((f32[8,2,128]{2,1,0:T(2,128)}, f32[8,2,128]{2,1,0:T(2,128)S(1)}, u32[]{:S(2)}, u32[]{:S(2)}) %collective-permute-start.1) | collective-permute-done | bytes 8224 | tf_op jit(solution)/shard_map/ppermute | solution.py:281
  37.9 7.6 %near.1 = f32[8,2,128]{2,1,0:T(2,128)} custom-call(f32[8,2,128]{2,1,0:T(2,128)} %cur.1, f32[8,2,128]{2,1,0:T(2,128)S(1)} %collective-permute-done.low, f32[8,2,128]{2,1,0:T(2,128)S(1)} %collective-permute-done.1.high, s32[8,8]{1,0:T(8,128)} %neighbours_h.1, s32[8]{0:T(128)} %count_h.1, f32[8,8,2,128,128]{4,3,2,1,0:T(8,128)} %blocks.1), custom_call_target="tpu_custom_call" | custom-call | flops 16777216 | bytes 8388608 | tf_op jit(solution)/shard_map/near/pallas_call | solution.py:42
  45.5 0.0 all-to-all-done.1.got
  45.5 0.6 %final.1 = (f32[1,2,2,256]{3,2,1,0:T(2,128)}, f32[1,2,2,96]{3,2,1,0:T(2,128)}) custom-call(f32[32,16,128]{2,1,0:T(8,128)S(1)} %all-to-all-done.1.got), custom_call_target="tpu_custom_call" | custom-call | flops 131072 | bytes 262144 | tf_op jit(solution)/shard_map/final/pallas_call | solution.py:42
Async XLA Ops:
  3.4 8.3 %all-to-all-start = ((f32[8,8,128]{2,1,0:T(8,128)}), f32[8,8,128]{2,1,0:T(8,128)S(1)}, u32[]{:S(2)}, u32[]{:S(2)}) async-start(f32[8,8,128]{2,1,0:T(8,128)} %leaf.1), calls=%async_computation | async-start | bytes 65536 | tf_op jit(solution)/shard_map/all_to_all | solution.py:275
  12.7 32.8 %all-to-all-start.1 = ((f32[32,16,128]{2,1,0:T(8,128)}), f32[32,16,128]{2,1,0:T(8,128)S(1)}, u32[]{:S(2)}, u32[]{:S(2)}) async-start(f32[32,16,128]{2,1,0:T(8,128)} %middle.1), calls=%async_computation.1 | async-start | bytes 524288 | tf_op jit(solution)/shard_map/all_to_all | solution.py:308
  22.6 8.7 %collective-permute-start = (f32[8,2,128]{2,1,0:T(2,128)}, f32[8,2,128]{2,1,0:T(2,128)S(1)}, u32[]{:S(2)}, u32[]{:S(2)}) collective-permute-start(f32[8,2,128]{2,1,0:T(2,128)} %cur.1), channel_id=1, source_target_pairs={{0,1},{1,2},{2,3},{3,4},{4,5},{5,6},{6,7},{7,8},{8,9},{9,10},{10,1... | collective-permute-start | bytes 24584 | tf_op jit(solution)/shard_map/ppermute | solution.py:280
  29.4 8.5 %collective-permute-start.1 = (f32[8,2,128]{2,1,0:T(2,128)}, f32[8,2,128]{2,1,0:T(2,128)S(1)}, u32[]{:S(2)}, u32[]{:S(2)}) collective-permute-start(f32[8,2,128]{2,1,0:T(2,128)} %cur.1), channel_id=1, source_target_pairs={{1,0},{2,1},{3,2},{4,3},{5,4},{6,5},{7,6},{8,7},{9,8},{10,9},{11,1... | collective-permute-start | bytes 24584 | tf_op jit(solution)/shard_map/ppermute | solution.py:281

commit v2 on v1

--- a/solution.py
+++ b/solution.py
@@ -41,7 +41,7 @@
     def placed(*operands):
         return run(
             *(
-                pltpu.with_memory_space_constraint(x, pltpu.HBM) if spec is HBM else x
+                x if spec is VMEM else pltpu.with_memory_space_constraint(x, spec.memory_space)
                 for x, spec in zip(operands, in_specs)
             )
         )
@@ -95,7 +95,7 @@
 def prep_kernel(
     src_low_h, op_low_h, cnt_low_h, src_up_h, op_up_h, cnt_up_h, tab_low_h, tab_up_h, phase_h, interp_h,
     wa, wb, ua, ub, rot, interp,
-    src_low, op_low, cnt_low, src_up, op_up, cnt_up, tab_low, tab_up, phase, code_v, code_s, sem, sems,
+    src_low, op_low, cnt_low, src_up, op_up, cnt_up, tab_low, tab_up, phase, ta, tb, code_v, code_s, sem, sems,
 ):
     clus, samp = place()
     copies = start_all(
@@ -106,19 +106,22 @@
         ],
         sems,
     )
-    for copy in copies:
+    for copy in copies[:6]:
         copy.wait()
     src = src_low[...]
     used = (rows_of(src.shape, 0) < cnt_low[...]) & ((src >> 3) == clus)
-    code = op_low[...] + 1
+    code = 64 - op_low[...]
     octant = src & 7
     for o in range(8):
-        code_v[pl.ds(o, 1), :] = jnp.sum(jnp.where(used & (octant == o), code, 0), axis=0, keepdims=True)
+        listed = jnp.sum(jnp.where(used & (octant == o), code, 0), axis=0, keepdims=True)
+        code_v[pl.ds(o, 1), :] = 64 - listed
     code_v[pl.ds(8, 8), :] = jnp.zeros((8, 256), jnp.int32)
     used_up = (rows_of(src_up.shape, 0) < cnt_up[...]) & (src_up[...] == clus)
     code_v[pl.ds(8, 1), pl.ds(0, 32)] = jnp.sum(jnp.where(used_up, op_up[...] + 1, 0), axis=0, keepdims=True)
-    copy = pltpu.make_async_copy(code_v, code_s, sem)
-    copy.start()
+    move = pltpu.make_async_copy(code_v, code_s, sem)
+    move.start()
+    for copy in copies[6:9]:
+        copy.wait()
     zero = jnp.zeros((8, 128), F32)
     row = rows_of((8, 128), 0)
     first_half = (row & 1) == 0
@@ -128,20 +131,27 @@
     rot[1] = zero
     rot[0, :, pl.ds(0, 96)] = jnp.cos(phase[...])
     rot[1, :, pl.ds(0, 96)] = jnp.sin(phase[...])
-    copy.wait()
+    ta[64] = zero
+    tb[64] = zero
+
+    def expand(n, carry):
+        parts = []
+        for c in range(2):
+            low = jnp.broadcast_to(tab_low[n, pl.ds(c, 1), pl.ds(0, 128)], (8, 128))
+            high = jnp.broadcast_to(tab_low[n, pl.ds(c, 1), pl.ds(128, 128)], (8, 128))
+            parts.append(jnp.where(first_half, low, high))
+        ta[n] = parts[0]
+        tb[n] = parts[1] * sign_low
+        return carry
+
+    lax.fori_loop(0, 64, expand, 0, unroll=8)
+    move.wait()
 
     def target(t, carry):
         for o in range(8):
-            i = code_s[o, t * 8 + samp]
-            n = jnp.maximum(i - 1, 0)
-            listed = jnp.where(i > 0, 1.0, 0.0).astype(F32)
-            parts = []
-            for c in range(2):
-                low = jnp.broadcast_to(tab_low[n, pl.ds(c, 1), pl.ds(0, 128)], (8, 128))
-                high = jnp.broadcast_to(tab_low[n, pl.ds(c, 1), pl.ds(128, 128)], (8, 128))
-                parts.append(jnp.where(first_half, low, high) * listed)
-            wa[t, o] = parts[0]
-            wb[t, o] = parts[1] * sign_low
+            n = code_s[o, t * 8 + samp]
+            wa[t, o] = ta[n]
+            wb[t, o] = tb[n]
         i = code_s[8, t]
         n = jnp.maximum(i - 1, 0)
         listed = jnp.where(i > 0, 1.0, 0.0).astype(F32)
@@ -151,10 +161,12 @@
         ub[t, :, pl.ds(0, 96)] = jnp.broadcast_to(tab_up[n, pl.ds(1, 1), :], (8, 96)) * listed * sign_up
         return carry
 
-    lax.fori_loop(0, 32, target, 0)
-
-
-def middle_kernel(got, interp, wa, wb, ua, ub, rot, out, upper):
+    lax.fori_loop(0, 32, target, 0, unroll=2)
+    for copy in copies[9:]:
+        copy.wait()
+
+
+def middle_kernel(got, interp, wa, wb, ua, ub, rot, arrived, out, upper):
     row = rows_of((8, 128), 0)
     halves = []
     for h in range(2):
@@ -173,7 +185,8 @@
         total = wa[t, 0] * plain[0] + wb[t, 0] * swapped[0]
         for o in range(1, 8):
             total += wa[t, o] * plain[o] + wb[t, o] * swapped[o]
-        out[t, pl.ds(0, 8), :] = total
+        out[3 * t] = total[:4]
+        out[3 * t + 1] = total[4:]
     upper[...] = jnp.zeros((8, 128), F32)
     cosine = rot[0][:, :96]
     sine = rot[1][:, :96]
@@ -185,72 +198,81 @@
     up = upper[...]
     up_swapped = jnp.where((row & 1) == 0, pltpu.roll(up, 7, 0), pltpu.roll(up, 1, 0))
     for t in range(32):
-        out[t, pl.ds(8, 8), :] = ua[t] * up + ub[t] * up_swapped
-
-
-def near_kernel(cur, low, high, neighbours_h, count_h, blocks, out, held, ext, acc, neighbours, count, sems):
+        out[3 * t + 2] = (ua[t] * up + ub[t] * up_swapped)[:4]
+
+
+def near_kernel(cur, even, odd, neighbours_h, count_h, blocks_h, out, blocks, ext, pieces, neighbours, count, sems):
     clus, samp = place()
     base = (clus * 8 + samp) * 8 - 8
-
-    def copy(b):
-        return pltpu.make_async_copy(blocks.at[b], held.at[b], sems.at[b])
+    lists = start_all(
+        [(cur, ext.at[pl.ds(8, 8)]), (neighbours_h, neighbours), (count_h, count)], sems.at[pl.ds(8, 3)]
+    )
+
+    def load(b):
+        return pltpu.make_async_copy(blocks_h.at[b], blocks.at[b], sems.at[b])
 
     for b in range(8):
-        copy(b).start()
-    lists = [
-        pltpu.make_async_copy(cur, ext.at[pl.ds(8, 8)], sems.at[8]),
-        pltpu.make_async_copy(neighbours_h, neighbours, sems.at[9]),
-        pltpu.make_async_copy(count_h, count, sems.at[10]),
-    ]
-    for one in lists:
-        one.start()
-    ext[pl.ds(0, 8)] = low[...]
-    ext[pl.ds(16, 8)] = high[...]
+        load(b).start()
+    parity = samp & 1
+    ext[pl.ds(16 * (1 - parity), 8)] = even[...]
+    ext[pl.ds(16 * parity, 8)] = odd[...]
+    pieces[...] = jnp.zeros((2, 256, 256), jnp.bfloat16)
+    ones = jnp.ones((16, 256), jnp.bfloat16)
     for one in lists:
         one.wait()
-    ones = jnp.ones((8, 128), F32)
+
+    def finish(slot, b):
+        summed = lax.dot_general(
+            ones, pieces[slot], (((1,), (1,)), ((), ())), preferred_element_type=F32
+        )
+        out[b, pl.ds(0, 1), :] = summed[0:1, :128]
+        out[b, pl.ds(1, 1), :] = summed[0:1, 128:]
 
     def box(b, carry):
+        slot = b & 1
+        finish(1 - slot, jnp.maximum(b - 1, 0))
         xs = []
         for k in range(8):
             i = neighbours[b, k] - base
             keep = jnp.where(k < count[b], 1.0, 0.0).astype(F32)
-            xr = jnp.broadcast_to(ext[i, pl.ds(0, 1), :], (8, 128)) * keep
-            xi = jnp.broadcast_to(ext[i, pl.ds(1, 1), :], (8, 128)) * keep
-            xs.append((xr, xi))
-        copy(b).wait()
-        for it in range(16):
-            re = None
-            for k, (xr, xi) in enumerate(xs):
-                br = held[b, k, 0, pl.ds(8 * it, 8), :]
-                bi = held[b, k, 1, pl.ds(8 * it, 8), :]
-                tr = br * xr - bi * xi
-                ti = br * xi + bi * xr
-                re, im = (tr, ti) if re is None else (re + tr, im + ti)
-            acc[0, pl.ds(8 * it, 8), :] = re
-            acc[1, pl.ds(8 * it, 8), :] = im
-        for c in range(2):
-            summed = lax.dot_general(
-                ones, acc[c], (((1,), (1,)), ((), ())), precision=HIGHEST, preferred_element_type=F32
-            )
-            out[b, pl.ds(c, 1), :] = summed[0:1]
+            xr = ext[i, pl.ds(0, 1), :] * keep
+            xi = ext[i, pl.ds(1, 1), :] * keep
+            xs.append((jnp.broadcast_to(xr, (8, 128)), jnp.broadcast_to(xi, (8, 128))))
+        load(b).wait()
+        for it in range(8):
+            halves = []
+            for half in range(2):
+                re = None
+                for k, (xr, xi) in enumerate(xs):
+                    br = blocks[b, k, 0, pl.ds(16 * it + 8 * half, 8), :]
+                    bi = blocks[b, k, 1, pl.ds(16 * it + 8 * half, 8), :]
+                    tr = br * xr - bi * xi
+                    ti = br * xi + bi * xr
+                    re, im = (tr, ti) if re is None else (re + tr, im + ti)
+                halves.append((re, im))
+            for c in range(2):
+                whole = jnp.concatenate([halves[0][c], halves[1][c]], axis=0)
+                high = whole.astype(jnp.bfloat16)
+                low = (whole - high.astype(F32)).astype(jnp.bfloat16)
+                pieces[slot, pl.ds(128 * c + 16 * it, 16), pl.ds(0, 128)] = high
+                pieces[slot, pl.ds(128 * c + 16 * it, 16), pl.ds(128, 128)] = low
         return carry
 
     lax.fori_loop(0, 8, box, 0)
+    finish(1, 7)
 
 
 def final_kernel(got, out_low, out_up):
-    low = got[0, pl.ds(0, 8), :]
-    up = got[0, pl.ds(8, 8), :]
+    sums = [got[k] for k in range(3)]
     for t in range(1, 32):
-        low += got[t, pl.ds(0, 8), :]
-        up += got[t, pl.ds(8, 8), :]
+        for k in range(3):
+            sums[k] += got[3 * t + k]
     for p in range(2):
         for c in range(2):
             k = 2 * p + c
             for h in range(2):
-                out_low[0, p, pl.ds(c, 1), pl.ds(128 * h, 128)] = low[2 * k + h : 2 * k + h + 1]
-            out_up[0, p, pl.ds(c, 1), :] = up[k : k + 1, :96]
+                out_low[0, p, pl.ds(c, 1), pl.ds(128 * h, 128)] = sums[p][2 * c + h : 2 * c + h + 1]
+            out_up[0, p, pl.ds(c, 1), :] = sums[2][k : k + 1, :96]
 
 
 def shape(*dims):
@@ -271,14 +293,10 @@
         ],
         flops=4 << 20, bytes_accessed=2 << 20, name="leaf",
     )(currents, radiation, interp_leaf, phase_leaf)
+    size = lax.axis_size(CLUS_SAMP)
     own, message = lax.optimization_barrier((currents, message))
+    even = lax.ppermute(own, CLUS_SAMP, [(i, i ^ 1) for i in range(size)])
     gathered = lax.all_to_all(message, SAMP, split_axis=0, concat_axis=0, tiled=True)
-
-    size = lax.axis_size(CLUS_SAMP)
-    up = [(i, i + 1) for i in range(size - 1)]
-    down = [(b, a) for a, b in up]
-    low = lax.ppermute(own, CLUS_SAMP, up)
-    high = lax.ppermute(own, CLUS_SAMP, down)
 
     wa, wb, ua, ub, rot, interp = call(
         prep_kernel,
@@ -291,6 +309,7 @@
             pltpu.VMEM((16, 256), jnp.int32), pltpu.VMEM((16, 256), jnp.int32), pltpu.VMEM((1, 256), jnp.int32),
             pltpu.VMEM((7, 32), jnp.int32), pltpu.VMEM((7, 32), jnp.int32), pltpu.VMEM((1, 32), jnp.int32),
             pltpu.VMEM((64, 2, 256), F32), pltpu.VMEM((64, 2, 96), F32), pltpu.VMEM((8, 96), F32),
+            pltpu.VMEM((65, 8, 128), F32), pltpu.VMEM((65, 8, 128), F32),
             pltpu.VMEM((16, 256), jnp.int32), pltpu.SMEM((16, 256), jnp.int32), pltpu.SemaphoreType.DMA,
             pltpu.SemaphoreType.DMA((10,)),
         ],
@@ -302,23 +321,25 @@
     )
 
     payload = call(
-        middle_kernel, shape(32, 16, 128), [VMEM] * 7, [pltpu.VMEM((8, 128), F32)],
+        middle_kernel, shape(96, 4, 128), [VMEM] * 8, [pltpu.VMEM((8, 128), F32)],
         flops=4 << 20, bytes_accessed=3 << 20, name="middle",
-    )(gathered.reshape(64, 128), interp, wa, wb, ua, ub, rot)
+    )(gathered.reshape(64, 128), interp, wa, wb, ua, ub, rot, even)
+    own, payload = lax.optimization_barrier((currents, payload))
     parts = lax.all_to_all(payload, CLUS, split_axis=0, concat_axis=0, tiled=True)
 
+    odd = lax.ppermute(own, CLUS_SAMP, [(i, ((i + 1) ^ 1) - 1) for i in range(1, size - 1)])
     near_field = call(
         near_kernel, shape(8, 2, 128), [HBM, VMEM, VMEM, HBM, HBM, HBM],
         [
             pltpu.VMEM((8, 8, 2, 128, 128), F32),
             pltpu.VMEM((24, 2, 128), F32),
-            pltpu.VMEM((2, 128, 128), F32),
+            pltpu.VMEM((2, 256, 256), jnp.bfloat16),
             pltpu.SMEM((8, 8), jnp.int32),
             pltpu.SMEM((8,), jnp.int32),
             pltpu.SemaphoreType.DMA((11,)),
         ],
         flops=16 << 20, bytes_accessed=8 << 20, name="near",
-    )(currents, low, high, neighbours, near_count, near_blocks)
+    )(currents, even, odd, neighbours, near_count, near_blocks)
 
     incoming_lower, incoming_upper = call(
         final_kernel, [shape(1, 2, 2, 256), shape(1, 2, 2, 96)], [VMEM],

time: 46.6 us -> 41.1 us (0.88)
  the two profiles are of different devices: /device:TPU:103 before, /device:TPU:8 now
where the time goes in v2:
time: 41.1 us; the launch traced here: 40.6 us
  starting transfers between devices  20.5 us (50%)
  Pallas kernels  11.5 us (28%)
  waiting for transfers between devices  7.91 us (19%)
  between operations  0.69 us (2%)
    all_to_all x1, starting transfers between devices, local(): lax.all_to_all(payload, CLUS, split_axis=0, concat_axis=0, tiled=True)  11.7 us
    pallas_call x5, Pallas kernels, placed(): run(*(x if spec is VMEM else pltpu.with_memory_space_constraint(x, spec.m...  11.5 us
    ppermute x1, waiting for transfers between devices, local(): lax.ppermute(own, CLUS_SAMP, [(i, (i + 1 ^ 1) - 1) for i in range(1, size...  5.39 us
    all_to_all x1, starting transfers between devices, local(): lax.all_to_all(message, SAMP, split_axis=0, concat_axis=0, tiled=True)  4.31 us
    ppermute x1, starting transfers between devices, local(): lax.ppermute(own, CLUS_SAMP, [(i, (i + 1 ^ 1) - 1) for i in range(1, size...  4.01 us
    all_to_all x1, waiting for transfers between devices, local(): lax.all_to_all(message, SAMP, split_axis=0, concat_axis=0, tiled=True)  2.52 us
  transfers between devices with their start and end apart: 4, of which 2 were waited for; matrix products, arithmetic and copies ran while one was open for 0% of the time, Pallas kernels for 17%

profile of v2, /device:TPU:8, one launch (start us, length us, event | category | flops | bytes accessed | tf_op | source)
XLA Modules:
  0.0 40.6 jit_solution(15247248283071943459)
XLA Ops:
  0.6 2.8 %leaf.1 = f32[8,8,128]{2,1,0:T(8,128)} custom-call(f32[8,2,128]{2,1,0:T(2,128)} %cur.1, f32[8,2,2,128,128]{4,3,2,1,0:T(8,128)} %rad_h.1, f32[128,256]{1,0:T(8,128)} %interp_h.1, f32[8,256]{1,0:T(8,128)} %phase_h.2), custom_call_target="tpu_custom_call" | custom-call | flops 4194304 | bytes 2097152 | tf_op jit(solution)/shard_map/leaf/pallas_call | solution.py:42
  3.4 4.3 %all-to-all-start = ((f32[8,8,128]{2,1,0:T(8,128)}), f32[8,8,128]{2,1,0:T(8,128)S(1)}, u32[]{:S(2)}, u32[]{:S(2)}) async-start(f32[8,8,128]{2,1,0:T(8,128)} %leaf.1), calls=%async_computation | async-start | bytes 65536 | tf_op jit(solution)/shard_map/all_to_all | solution.py:299
  7.7 0.5 %collective-permute-start = (f32[8,2,128]{2,1,0:T(2,128)}, f32[8,2,128]{2,1,0:T(2,128)S(1)}, u32[]{:S(2)}, u32[]{:S(2)}) collective-permute-start(f32[8,2,128]{2,1,0:T(2,128)} %cur.1), channel_id=1, source_target_pairs={{0,1},{1,0},{2,3},{3,2},{4,5},{5,4},{6,7},{7,6},{8,9},{9,8},{10,11... | collective-permute-start | bytes 24584 | tf_op jit(solution)/shard_map/ppermute | solution.py:298
  8.2 2.4 %prep.1 = (f32[32,8,8,128]{3,2,1,0:T(8,128)S(1)}, f32[32,8,8,128]{3,2,1,0:T(8,128)S(1)}, f32[32,8,128]{2,1,0:T(8,128)S(1)}, f32[32,8,128]{2,1,0:T(8,128)S(1)}, f...) custom-call(s32[16,256]{1,0:T(8,128)} %bitcast.10, s32[16,256]{1,0:T(8,128)} %bitcast.11, s32[1,256]{1,0:T(1,128)} %bitcast.14, ...), custom_call_target="tpu_custom_call" | custom-call | flops 1048576 | bytes 4194304 | tf_op jit(solution)/shard_map/prep/pallas_call | solution.py:42
  10.6 0.0 collective-permute-done.arrived.even
  10.6 2.5 %all-to-all-done = f32[8,8,128]{2,1,0:T(8,128)S(1)} async-done(((f32[8,8,128]{2,1,0:T(8,128)}), f32[8,8,128]{2,1,0:T(8,128)S(1)}, u32[]{:S(2)}, u32[]{:S(2)}) %all-to-all-start) | async-done | bytes 32800 | tf_op jit(solution)/shard_map/all_to_all | solution.py:299
  13.2 1.0 %middle.1 = f32[96,4,128]{2,1,0:T(4,128)} custom-call(f32[64,128]{1,0:T(8,128)S(1)} %bitcast.8, f32[96,256]{1,0:T(8,128)S(1)} %get-tuple-element.17.interp, f32[32,8,8,128]{3,2,1,0:T(8,128)S(1)} %get-tuple-element.18.wa, f32[32,8,8,128]{3,2,1,0:T(8,128)S(1)} %get-tuple-element.19.wb, f32[32,8,128]{2,1,0:T(8,128)S(1)} %get-tuple-element.20.ua, ...), custom_call_target="tpu_custom_call" | custom-call | flops 4194304 | bytes 3145728 | tf_op jit(solution)/shard_map/middle/pallas_call | solution.py:42
  14.1 11.7 %all-to-all-start.1 = ((f32[96,4,128]{2,1,0:T(4,128)}), f32[96,4,128]{2,1,0:T(4,128)S(1)}, u32[]{:S(2)}, u32[]{:S(2)}) async-start(f32[96,4,128]{2,1,0:T(4,128)} %middle.1), calls=%async_computation.1 | async-start | bytes 393216 | tf_op jit(solution)/shard_map/all_to_all | solution.py:328
  25.9 4.0 %collective-permute-start.1 = (f32[8,2,128]{2,1,0:T(2,128)}, f32[8,2,128]{2,1,0:T(2,128)S(1)}, u32[]{:S(2)}, u32[]{:S(2)}) collective-permute-start(f32[8,2,128]{2,1,0:T(2,128)} %cur.1), channel_id=1, source_target_pairs={{1,2},{2,1},{3,4},{4,3},{5,6},{6,5},{7,8},{8,7},{9,10},{10,9},{11,... | collective-permute-start | bytes 24584 | tf_op jit(solution)/shard_map/ppermute | solution.py:330
  29.9 5.4 %collective-permute-done.1.odd = f32[8,2,128]{2,1,0:T(2,128)S(1)} collective-permute-done((f32[8,2,128]{2,1,0:T(2,128)}, f32[8,2,128]{2,1,0:T(2,128)S(1)}, u32[]{:S(2)}, u32[]{:S(2)}) %collective-permute-start.1) | collective-permute-done | bytes 8224 | tf_op jit(solution)/shard_map/ppermute | solution.py:330
  35.3 4.7 %near.1 = f32[8,2,128]{2,1,0:T(2,128)} custom-call(f32[8,2,128]{2,1,0:T(2,128)} %cur.1, f32[8,2,128]{2,1,0:T(2,128)S(1)} %collective-permute-done.arrived.even, f32[8,2,128]{2,1,0:T(2,128)S(1)} %collective-permute-done.1.odd, s32[8,8]{1,0:T(8,128)} %neighbours_h.1, s32[8]{0:T(128)} %count_h.1, f32[8,8,2,128,128]{4,3,2,1,0:T(8,128)} %blocks_h.1), custom_call_target="tpu_custom_call" | custom-call | flops 16777216 | bytes 8388608 | tf_op jit(solution)/shard_map/near/pallas_call | solution.py:42
  39.9 0.0 all-to-all-done.1.got
  40.0 0.6 %final.1 = (f32[1,2,2,256]{3,2,1,0:T(2,128)}, f32[1,2,2,96]{3,2,1,0:T(2,128)}) custom-call(f32[96,4,128]{2,1,0:T(4,128)S(1)} %all-to-all-done.1.got), custom_call_target="tpu_custom_call" | custom-call | flops 131072 | bytes 262144 | tf_op jit(solution)/shard_map/final/pallas_call | solution.py:42
Async XLA Ops:
  3.4 9.8 %all-to-all-start = ((f32[8,8,128]{2,1,0:T(8,128)}), f32[8,8,128]{2,1,0:T(8,128)S(1)}, u32[]{:S(2)}, u32[]{:S(2)}) async-start(f32[8,8,128]{2,1,0:T(8,128)} %leaf.1), calls=%async_computation | async-start | bytes 65536 | tf_op jit(solution)/shard_map/all_to_all | solution.py:299
  7.7 2.9 %collective-permute-start = (f32[8,2,128]{2,1,0:T(2,128)}, f32[8,2,128]{2,1,0:T(2,128)S(1)}, u32[]{:S(2)}, u32[]{:S(2)}) collective-permute-start(f32[8,2,128]{2,1,0:T(2,128)} %cur.1), channel_id=1, source_target_pairs={{0,1},{1,0},{2,3},{3,2},{4,5},{5,4},{6,7},{7,6},{8,9},{9,8},{10,11... | collective-permute-start | bytes 24584 | tf_op jit(solution)/shard_map/ppermute | solution.py:298
  14.1 25.8 %all-to-all-start.1 = ((f32[96,4,128]{2,1,0:T(4,128)}), f32[96,4,128]{2,1,0:T(4,128)S(1)}, u32[]{:S(2)}, u32[]{:S(2)}) async-start(f32[96,4,128]{2,1,0:T(4,128)} %middle.1), calls=%async_computation.1 | async-start | bytes 393216 | tf_op jit(solution)/shard_map/all_to_all | solution.py:328
  25.9 9.4 %collective-permute-start.1 = (f32[8,2,128]{2,1,0:T(2,128)}, f32[8,2,128]{2,1,0:T(2,128)S(1)}, u32[]{:S(2)}, u32[]{:S(2)}) collective-permute-start(f32[8,2,128]{2,1,0:T(2,128)} %cur.1), channel_id=1, source_target_pairs={{1,2},{2,1},{3,4},{4,3},{5,6},{6,5},{7,8},{8,7},{9,10},{10,9},{11,... | collective-permute-start | bytes 24584 | tf_op jit(solution)/shard_map/ppermute | solution.py:330

commit v3 on v2

--- a/solution.py
+++ b/solution.py
@@ -166,7 +166,7 @@
         copy.wait()
 
 
-def middle_kernel(got, interp, wa, wb, ua, ub, rot, arrived, out, upper):
+def middle_kernel(got, interp, wa, wb, ua, ub, rot, even, odd, out, upper):
     row = rows_of((8, 128), 0)
     halves = []
     for h in range(2):
@@ -296,6 +296,7 @@
     size = lax.axis_size(CLUS_SAMP)
     own, message = lax.optimization_barrier((currents, message))
     even = lax.ppermute(own, CLUS_SAMP, [(i, i ^ 1) for i in range(size)])
+    odd = lax.ppermute(own, CLUS_SAMP, [(i, ((i + 1) ^ 1) - 1) for i in range(1, size - 1)])
     gathered = lax.all_to_all(message, SAMP, split_axis=0, concat_axis=0, tiled=True)
 
     wa, wb, ua, ub, rot, interp = call(
@@ -321,13 +322,11 @@
     )
 
     payload = call(
-        middle_kernel, shape(96, 4, 128), [VMEM] * 8, [pltpu.VMEM((8, 128), F32)],
+        middle_kernel, shape(96, 4, 128), [VMEM] * 9, [pltpu.VMEM((8, 128), F32)],
         flops=4 << 20, bytes_accessed=3 << 20, name="middle",
-    )(gathered.reshape(64, 128), interp, wa, wb, ua, ub, rot, even)
-    own, payload = lax.optimization_barrier((currents, payload))
+    )(gathered.reshape(64, 128), interp, wa, wb, ua, ub, rot, even, odd)
     parts = lax.all_to_all(payload, CLUS, split_axis=0, concat_axis=0, tiled=True)
 
-    odd = lax.ppermute(own, CLUS_SAMP, [(i, ((i + 1) ^ 1) - 1) for i in range(1, size - 1)])
     near_field = call(
         near_kernel, shape(8, 2, 128), [HBM, VMEM, VMEM, HBM, HBM, HBM],
         [

time: 41.1 us -> 40.7 us (level)
  the two profiles are of different devices: /device:TPU:8 before, /device:TPU:32 now
where the time goes in v3:
time: 40.7 us; the launch traced here: 40.3 us
  starting transfers between devices  22.2 us (55%)
  Pallas kernels  11.5 us (28%)
  waiting for transfers between devices  5.87 us (14%)
  between operations  0.7 us (2%)
    all_to_all x1, starting transfers between devices, local(): lax.all_to_all(payload, CLUS, split_axis=0, concat_axis=0, tiled=True)  12.4 us
    pallas_call x5, Pallas kernels, placed(): run(*(x if spec is VMEM else pltpu.with_memory_space_constraint(x, spec.m...  11.5 us
    all_to_all x1, waiting for transfers between devices, local(): lax.all_to_all(payload, CLUS, split_axis=0, concat_axis=0, tiled=True)  5.86 us
    ppermute x1, starting transfers between devices, local(): lax.ppermute(own, CLUS_SAMP, [(i, (i + 1 ^ 1) - 1) for i in range(1, size...  4.96 us
    all_to_all x1, starting transfers between devices, local(): lax.all_to_all(message, SAMP, split_axis=0, concat_axis=0, tiled=True)  4.31 us
  transfers between devices with their start and end apart: 4, of which 1 were waited for; matrix products, arithmetic and copies ran while one was open for 0% of the time, Pallas kernels for 18%

profile of v3, /device:TPU:32, one launch (start us, length us, event | category | flops | bytes accessed | tf_op | source)
XLA Modules:
  0.0 40.3 jit_solution(1197531710453613012)
XLA Ops:
  0.6 2.8 %leaf.1 = f32[8,8,128]{2,1,0:T(8,128)} custom-call(f32[8,2,128]{2,1,0:T(2,128)} %cur.1, f32[8,2,2,128,128]{4,3,2,1,0:T(8,128)} %rad_h.1, f32[128,256]{1,0:T(8,128)} %interp_h.1, f32[8,256]{1,0:T(8,128)} %phase_h.2), custom_call_target="tpu_custom_call" | custom-call | flops 4194304 | bytes 2097152 | tf_op jit(solution)/shard_map/leaf/pallas_call | solution.py:42
  3.4 4.3 %all-to-all-start = ((f32[8,8,128]{2,1,0:T(8,128)}), f32[8,8,128]{2,1,0:T(8,128)S(1)}, u32[]{:S(2)}, u32[]{:S(2)}) async-start(f32[8,8,128]{2,1,0:T(8,128)} %leaf.1), calls=%async_computation | async-start | bytes 65536 | tf_op jit(solution)/shard_map/all_to_all | solution.py:300
  7.7 0.5 %collective-permute-start = (f32[8,2,128]{2,1,0:T(2,128)}, f32[8,2,128]{2,1,0:T(2,128)S(1)}, u32[]{:S(2)}, u32[]{:S(2)}) collective-permute-start(f32[8,2,128]{2,1,0:T(2,128)} %cur.1), channel_id=1, source_target_pairs={{0,1},{1,0},{2,3},{3,2},{4,5},{5,4},{6,7},{7,6},{8,9},{9,8},{10,11... | collective-permute-start | bytes 24584 | tf_op jit(solution)/shard_map/ppermute | solution.py:298
  8.2 5.0 %collective-permute-start.1 = (f32[8,2,128]{2,1,0:T(2,128)}, f32[8,2,128]{2,1,0:T(2,128)S(1)}, u32[]{:S(2)}, u32[]{:S(2)}) collective-permute-start(f32[8,2,128]{2,1,0:T(2,128)} %cur.1), channel_id=1, source_target_pairs={{1,2},{2,1},{3,4},{4,3},{5,6},{6,5},{7,8},{8,7},{9,10},{10,9},{11,... | collective-permute-start | bytes 24584 | tf_op jit(solution)/shard_map/ppermute | solution.py:299
  13.2 2.4 %prep.1 = (f32[32,8,8,128]{3,2,1,0:T(8,128)S(1)}, f32[32,8,8,128]{3,2,1,0:T(8,128)S(1)}, f32[32,8,128]{2,1,0:T(8,128)S(1)}, f32[32,8,128]{2,1,0:T(8,128)S(1)}, f...) custom-call(s32[16,256]{1,0:T(8,128)} %bitcast.10, s32[16,256]{1,0:T(8,128)} %bitcast.11, s32[1,256]{1,0:T(1,128)} %bitcast.14, ...), custom_call_target="tpu_custom_call" | custom-call | flops 1048576 | bytes 4194304 | tf_op jit(solution)/shard_map/prep/pallas_call | solution.py:42
  15.6 0.0 collective-permute-done.even
  15.6 0.0 collective-permute-done.1.odd
  15.6 0.0 all-to-all-done
  15.6 1.0 %middle.1 = f32[96,4,128]{2,1,0:T(4,128)} custom-call(f32[64,128]{1,0:T(8,128)S(1)} %bitcast.8, f32[96,256]{1,0:T(8,128)S(1)} %get-tuple-element.15.interp, f32[32,8,8,128]{3,2,1,0:T(8,128)S(1)} %get-tuple-element.16.wa, f32[32,8,8,128]{3,2,1,0:T(8,128)S(1)} %get-tuple-element.17.wb, f32[32,8,128]{2,1,0:T(8,128)S(1)} %get-tuple-element.18.ua, ...), custom_call_target="tpu_custom_call" | custom-call | flops 4194304 | bytes 3145728 | tf_op jit(solution)/shard_map/middle/pallas_call | solution.py:42
  16.6 12.4 %all-to-all-start.1 = ((f32[96,4,128]{2,1,0:T(4,128)}), f32[96,4,128]{2,1,0:T(4,128)S(1)}, u32[]{:S(2)}, u32[]{:S(2)}) async-start(f32[96,4,128]{2,1,0:T(4,128)} %middle.1), calls=%async_computation.1 | async-start | bytes 393216 | tf_op jit(solution)/shard_map/all_to_all | solution.py:328
  29.1 4.7 %near.1 = f32[8,2,128]{2,1,0:T(2,128)} custom-call(f32[8,2,128]{2,1,0:T(2,128)} %cur.1, f32[8,2,128]{2,1,0:T(2,128)S(1)} %collective-permute-done.even, f32[8,2,128]{2,1,0:T(2,128)S(1)} %collective-permute-done.1.odd, s32[8,8]{1,0:T(8,128)} %neighbours_h.1, s32[8]{0:T(128)} %count_h.1, f32[8,8,2,128,128]{4,3,2,1,0:T(8,128)} %blocks_h.1), custom_call_target="tpu_custom_call" | custom-call | flops 16777216 | bytes 8388608 | tf_op jit(solution)/shard_map/near/pallas_call | solution.py:42
  33.8 5.9 %all-to-all-done.1.got = f32[96,4,128]{2,1,0:T(4,128)S(1)} async-done(((f32[96,4,128]{2,1,0:T(4,128)}), f32[96,4,128]{2,1,0:T(4,128)S(1)}, u32[]{:S(2)}, u32[]{:S(2)}) %all-to-all-start.1) | async-done | bytes 196640 | tf_op jit(solution)/shard_map/all_to_all | solution.py:328
  39.6 0.6 %final.1 = (f32[1,2,2,256]{3,2,1,0:T(2,128)}, f32[1,2,2,96]{3,2,1,0:T(2,128)}) custom-call(f32[96,4,128]{2,1,0:T(4,128)S(1)} %all-to-all-done.1.got), custom_call_target="tpu_custom_call" | custom-call | flops 131072 | bytes 262144 | tf_op jit(solution)/shard_map/final/pallas_call | solution.py:42
Async XLA Ops:
  3.4 12.2 %all-to-all-start = ((f32[8,8,128]{2,1,0:T(8,128)}), f32[8,8,128]{2,1,0:T(8,128)S(1)}, u32[]{:S(2)}, u32[]{:S(2)}) async-start(f32[8,8,128]{2,1,0:T(8,128)} %leaf.1), calls=%async_computation | async-start | bytes 65536 | tf_op jit(solution)/shard_map/all_to_all | solution.py:300
  7.7 7.9 %collective-permute-start = (f32[8,2,128]{2,1,0:T(2,128)}, f32[8,2,128]{2,1,0:T(2,128)S(1)}, u32[]{:S(2)}, u32[]{:S(2)}) collective-permute-start(f32[8,2,128]{2,1,0:T(2,128)} %cur.1), channel_id=1, source_target_pairs={{0,1},{1,0},{2,3},{3,2},{4,5},{5,4},{6,7},{7,6},{8,9},{9,8},{10,11... | collective-permute-start | bytes 24584 | tf_op jit(solution)/shard_map/ppermute | solution.py:298
  8.2 7.4 %collective-permute-start.1 = (f32[8,2,128]{2,1,0:T(2,128)}, f32[8,2,128]{2,1,0:T(2,128)S(1)}, u32[]{:S(2)}, u32[]{:S(2)}) collective-permute-start(f32[8,2,128]{2,1,0:T(2,128)} %cur.1), channel_id=1, source_target_pairs={{1,2},{2,1},{3,4},{4,3},{5,6},{6,5},{7,8},{8,7},{9,10},{10,9},{11,... | collective-permute-start | bytes 24584 | tf_op jit(solution)/shard_map/ppermute | solution.py:299
  16.6 23.0 %all-to-all-start.1 = ((f32[96,4,128]{2,1,0:T(4,128)}), f32[96,4,128]{2,1,0:T(4,128)S(1)}, u32[]{:S(2)}, u32[]{:S(2)}) async-start(f32[96,4,128]{2,1,0:T(4,128)} %middle.1), calls=%async_computation.1 | async-start | bytes 393216 | tf_op jit(solution)/shard_map/all_to_all | solution.py:328

commit v4 on v3

v4 whole, which is shorter than its diff:
```python
import jax
import jax.numpy as jnp
from jax import lax
from jax.experimental import pallas as pl
from jax.experimental.pallas import tpu as pltpu
from jax.sharding import Mesh
from jax.sharding import PartitionSpec as P

CLUS = ("clus_0", "clus_1")
SAMP = ("samp_0", "samp_1")
CLUS_SAMP = CLUS + SAMP

F32 = jnp.float32
BF16 = jnp.bfloat16
VMEM = pl.BlockSpec(memory_space=pltpu.VMEM)
SMEM = pl.BlockSpec(memory_space=pltpu.SMEM)
HBM = pl.BlockSpec(memory_space=pltpu.HBM)


def place():
    clus = lax.axis_index("clus_0") * 8 + lax.axis_index("clus_1")
    samp = lax.axis_index("samp_0") * 2 + lax.axis_index("samp_1")
    return clus, samp


def call(kernel, outs, in_specs, scratch=(), mib=16, flops=0, bytes_accessed=0):
    many = isinstance(outs, (list, tuple))
    run = pl.pallas_call(
        kernel,
        out_shape=outs,
        in_specs=in_specs,
        out_specs=[VMEM] * len(outs) if many else VMEM,
        scratch_shapes=list(scratch),
        compiler_params=pltpu.CompilerParams(vmem_limit_bytes=mib << 20),
        cost_estimate=pl.CostEstimate(flops=flops, bytes_accessed=bytes_accessed, transcendentals=0),
    )

    def placed(*operands):
        return run(
            *(
                x if spec is VMEM else pltpu.with_memory_space_constraint(x, spec.memory_space)
                for x, spec in zip(operands, in_specs)
            )
        )

    return placed


def rows_of(shape, axis):
    return lax.broadcasted_iota(jnp.int32, shape, axis)


def start_all(pairs, sems):
    copies = [pltpu.make_async_copy(a, b, sems.at[i]) for i, (a, b) in enumerate(pairs)]
    for copy in copies:
        copy.start()
    return copies


def pieces_of(x):
    high = x.astype(BF16)
    return high, (x - high.astype(F32)).astype(BF16)


def rotated(cosine, sine, y, p):
    yr = y[16 * p : 16 * p + 8]
    yi = y[16 * p + 8 : 16 * p + 16]
    re = jnp.sum(cosine * yr - sine * yi, axis=0, keepdims=True)
    im = jnp.sum(sine * yr + cosine * yi, axis=0, keepdims=True)
    return re, im


def leaf_kernel(
    cur_h, rad_h, interp_h, phase_h, src_low_h, op_low_h, cnt_low_h, src_up_h, op_up_h, cnt_up_h,
    tab_low_h, tab_up_h, phase_up_h, interp_up_h,
    out, code_v, ta, tb, tab_up, rot, weights,
    cur, rad, interp, phase, src_low, op_low, cnt_low, src_up, op_up, cnt_up, tab_low, phase_up, interp_up,
    pat, msg, sems,
):
    clus, _ = place()
    copies = start_all(
        [
            (src_low_h, src_low), (op_low_h, op_low), (cnt_low_h, cnt_low), (src_up_h, src_up),
            (op_up_h, op_up), (cnt_up_h, cnt_up), (cur_h, cur), (phase_h, phase), (interp_h, interp),
            (tab_low_h, tab_low), (tab_up_h, tab_up), (phase_up_h, phase_up), (interp_up_h, interp_up),
        ]
        + [(rad_h.at[b], rad.at[b]) for b in range(8)],
        sems,
    )
    for copy in copies[:13]:
        copy.wait()
    zero = jnp.zeros((8, 128), F32)
    row = rows_of((8, 128), 0)
    first_half = (row & 1) == 0
    sign_low = jnp.where((row & 2) == 0, -1.0, 1.0).astype(F32)
    src = src_low[...]
    used = (rows_of(src.shape, 0) < cnt_low[...]) & ((src >> 3) == clus)
    code = 64 - op_low[...]
    octant = src & 7
    for o in range(8):
        listed = jnp.sum(jnp.where(used & (octant == o), code, 0), axis=0, keepdims=True)
        code_v[pl.ds(o, 1), :] = 64 - listed
    code_v[pl.ds(8, 8), :] = jnp.zeros((8, 256), jnp.int32)
    used_up = (rows_of(src_up.shape, 0) < cnt_up[...]) & (src_up[...] == clus)
    code_v[pl.ds(8, 1), pl.ds(0, 32)] = jnp.sum(jnp.where(used_up, op_up[...] + 1, 0), axis=0, keepdims=True)
    ta[64] = zero
    tb[64] = zero

    def expand(n, carry):
        parts = []
        for c in range(2):
            low = jnp.broadcast_to(tab_low[n, pl.ds(c, 1), pl.ds(0, 128)], (8, 128))
            high = jnp.broadcast_to(tab_low[n, pl.ds(c, 1), pl.ds(128, 128)], (8, 128))
            parts.append(jnp.where(first_half, low, high))
        ta[n] = parts[0]
        tb[n] = parts[1] * sign_low
        return carry

    lax.fori_loop(0, 64, expand, 0, unroll=8)
    rot[0] = zero
    rot[1] = zero
    rot[0, :, pl.ds(0, 96)] = jnp.cos(phase_up[...])
    rot[1, :, pl.ds(0, 96)] = jnp.sin(phase_up[...])
    high, low = pieces_of(interp_up[...])
    weights[...] = jnp.concatenate([high, low, high], axis=1)
    high, low = pieces_of(interp[...])
    weights_leaf = jnp.concatenate([high, low, high], axis=0)
    cosine = jnp.cos(phase[...])
    sine = jnp.sin(phase[...])
    own = cur[...].reshape(16, 128)
    for peer in range(8):
        out[peer, pl.ds(8, 16), :] = own
    columns = own.T
    for b in range(8):
        copies[13 + b].wait()
        cr = jnp.broadcast_to(columns[:, 2 * b : 2 * b + 1], (128, 128))
        ci = jnp.broadcast_to(columns[:, 2 * b + 1 : 2 * b + 2], (128, 128))
        for p in range(2):
            rr = rad[b, p, 0]
            ri = rad[b, p, 1]
            pat[pl.ds(16 * p + b, 1), :] = jnp.sum(rr * cr - ri * ci, axis=0, keepdims=True)
            pat[pl.ds(16 * p + 8 + b, 1), :] = jnp.sum(rr * ci + ri * cr, axis=0, keepdims=True)
    high, low = pieces_of(pat[...])
    lifted = jnp.dot(
        jnp.concatenate([high, high, low], axis=1), weights_leaf, preferred_element_type=F32
    )
    for p in range(2):
        for c, part in enumerate(rotated(cosine, sine, lifted, p)):
            for h in range(2):
                msg[pl.ds(4 * p + 2 * c + h, 1), :] = part[:, 128 * h : 128 * h + 128]
    whole = msg[...]
    for peer in range(8):
        out[peer, pl.ds(0, 8), :] = whole


def prep_kernel(code_v, ta, tb, tab_up, wa, wb, ua, ub, code_s, sem):
    _, samp = place()
    move = pltpu.make_async_copy(code_v, code_s, sem)
    move.start()
    row = rows_of((8, 128), 0)
    sign_up = jnp.where((row & 1) == 0, -1.0, 1.0).astype(F32)[:, :96]
    ua[...] = jnp.zeros((32, 8, 128), F32)
    ub[...] = jnp.zeros((32, 8, 128), F32)
    move.wait()

    def target(t, carry):
        for o in range(8):
            n = code_s[o, t * 8 + samp]
            wa[t, o] = ta[n]
            wb[t, o] = tb[n]
        i = code_s[8, t]
        n = jnp.maximum(i - 1, 0)
        listed = jnp.where(i > 0, 1.0, 0.0).astype(F32)
        ua[t, :, pl.ds(0, 96)] = jnp.broadcast_to(tab_up[n, pl.ds(0, 1), :], (8, 96)) * listed
        ub[t, :, pl.ds(0, 96)] = jnp.broadcast_to(tab_up[n, pl.ds(1, 1), :], (8, 96)) * listed * sign_up
        return carry

    lax.fori_loop(0, 32, target, 0, unroll=2)


def middle_kernel(got, weights, wa, wb, ua, ub, rot, out, upper):
    row = rows_of((8, 128), 0)
    halves = []
    for h in range(2):
        halves.append(
            jnp.concatenate([got[pl.ds(2 * k + h, 8, stride=24), :] for k in range(4)], axis=0)
        )
    high, low = pieces_of(jnp.concatenate(halves, axis=1))
    lifted = lax.dot_general(
        jnp.concatenate([high, high, low], axis=1), weights[...], (((1,), (1,)), ((), ())),
        preferred_element_type=F32,
    )
    plain = [got[pl.ds(24 * o, 8), :] for o in range(8)]
    swapped = [
        jnp.where((row & 2) == 0, pltpu.roll(x, 6, 0), pltpu.roll(x, 2, 0)) for x in plain
    ]
    for t in range(32):
        total = wa[t, 0] * plain[0] + wb[t, 0] * swapped[0]
        for o in range(1, 8):
            total += wa[t, o] * plain[o] + wb[t, o] * swapped[o]
        out[3 * t] = total[:4]
        out[3 * t + 1] = total[4:]
    upper[...] = jnp.zeros((8, 128), F32)
    cosine = rot[0][:, :96]
    sine = rot[1][:, :96]
    for p in range(2):
        for c, part in enumerate(rotated(cosine, sine, lifted, p)):
            upper[pl.ds(2 * p + c, 1), pl.ds(0, 96)] = part
    up = upper[...]
    up_swapped = jnp.where((row & 1) == 0, pltpu.roll(up, 7, 0), pltpu.roll(up, 1, 0))
    for t in range(32):
        out[3 * t + 2] = (ua[t] * up + ub[t] * up_swapped)[:4]


def near_kernel(got, cross, neighbours_h, count_h, blocks_h, out, blocks, ext, pieces, neighbours, count, sems):
    clus, samp = place()
    base = (clus * 8 + samp) * 8 - 8
    lists = start_all([(neighbours_h, neighbours), (count_h, count)], sems.at[pl.ds(8, 2)])

    def load(b):
        return pltpu.make_async_copy(blocks_h.at[b], blocks.at[b], sems.at[b])

    for b in range(8):
        load(b).start()
    outside = cross[...].reshape(16, 128)
    before = got[jnp.maximum(samp - 1, 0), pl.ds(8, 16), :]
    after = got[jnp.minimum(samp + 1, 7), pl.ds(8, 16), :]
    ext[pl.ds(0, 16), :] = jnp.where(samp > 0, before, outside)
    ext[pl.ds(16, 16), :] = got[samp, pl.ds(8, 16), :]
    ext[pl.ds(32, 16), :] = jnp.where(samp < 7, after, outside)
    pieces[...] = jnp.zeros((2, 256, 256), BF16)
    ones = jnp.ones((16, 256), BF16)
    for one in lists:
        one.wait()

    def finish(slot, b):
        summed = lax.dot_general(
            ones, pieces[slot], (((1,), (1,)), ((), ())), preferred_element_type=F32
        )
        out[b, pl.ds(0, 1), :] = summed[0:1, :128]
        out[b, pl.ds(1, 1), :] = summed[0:1, 128:]

    def box(b, carry):
        slot = b & 1
        finish(1 - slot, jnp.maximum(b - 1, 0))
        xs = []
        for k in range(8):
            i = neighbours[b, k] - base
            keep = jnp.where(k < count[b], 1.0, 0.0).astype(F32)
            xr = ext[pl.ds(2 * i, 1), :] * keep
            xi = ext[pl.ds(2 * i + 1, 1), :] * keep
            xs.append((jnp.broadcast_to(xr, (8, 128)), jnp.broadcast_to(xi, (8, 128))))
        load(b).wait()
        for it in range(8):
            halves = []
            for half in range(2):
                re = None
                for k, (xr, xi) in enumerate(xs):
                    br = blocks[b, k, 0, pl.ds(16 * it + 8 * half, 8), :]
                    bi = blocks[b, k, 1, pl.ds(16 * it + 8 * half, 8), :]
                    tr = br * xr - bi * xi
                    ti = br * xi + bi * xr
                    re, im = (tr, ti) if re is None else (re + tr, im + ti)
                halves.append((re, im))
            for c in range(2):
                whole = jnp.concatenate([halves[0][c], halves[1][c]], axis=0)
                high = whole.astype(BF16)
                low = (whole - high.astype(F32)).astype(BF16)
                pieces[slot, pl.ds(128 * c + 16 * it, 16), pl.ds(0, 128)] = high
                pieces[slot, pl.ds(128 * c + 16 * it, 16), pl.ds(128, 128)] = low
        return carry

    lax.fori_loop(0, 8, box, 0)
    finish(1, 7)


def final_kernel(got, out_low, out_up):
    sums = [got[k] for k in range(3)]
    for t in range(1, 32):
        for k in range(3):
            sums[k] += got[3 * t + k]
    for p in range(2):
        for c in range(2):
            k = 2 * p + c
            for h in range(2):
                out_low[0, p, pl.ds(c, 1), pl.ds(128 * h, 128)] = sums[p][2 * c + h : 2 * c + h + 1]
            out_up[0, p, pl.ds(c, 1), :] = sums[2][k : k + 1, :96]


def shape(*dims):
    return jax.ShapeDtypeStruct(dims, F32)


def local(
    currents, near_blocks, neighbours, near_count, radiation, interp_leaf, phase_leaf,
    interp_upper, phase_upper, tables_lower, operator_lower, sources_lower, count_lower,
    tables_upper, operator_upper, sources_upper, count_upper,
):
    ints = jnp.int32
    message, code, ta, tb, tab_up, rot, weights = call(
        leaf_kernel,
        [
            shape(8, 24, 128), jax.ShapeDtypeStruct((16, 256), ints), shape(65, 8, 128), shape(65, 8, 128),
            shape(64, 2, 96), shape(2, 8, 128), jax.ShapeDtypeStruct((96, 768), BF16),
        ],
        [HBM] * 14,
        [
            pltpu.VMEM((8, 2, 128), F32), pltpu.VMEM((8, 2, 2, 128, 128), F32),
            pltpu.VMEM((128, 256), F32), pltpu.VMEM((8, 256), F32),
            pltpu.VMEM((16, 256), ints), pltpu.VMEM((16, 256), ints), pltpu.VMEM((1, 256), ints),
            pltpu.VMEM((7, 32), ints), pltpu.VMEM((7, 32), ints), pltpu.VMEM((1, 32), ints),
            pltpu.VMEM((64, 2, 256), F32), pltpu.VMEM((8, 96), F32), pltpu.VMEM((96, 256), F32),
            pltpu.VMEM((32, 128), F32), pltpu.VMEM((8, 128), F32), pltpu.SemaphoreType.DMA((21,)),
        ],
        flops=4 << 20, bytes_accessed=3 << 20,
    )(
        currents, radiation, interp_leaf, phase_leaf,
        sources_lower.T, operator_lower.T, count_lower.reshape(1, -1),
        sources_upper.T, operator_upper.T, count_upper.reshape(1, -1),
        tables_lower, tables_upper, phase_upper, interp_upper.T,
    )
    own, message = lax.optimization_barrier((currents, message))
    gathered = lax.all_to_all(message, SAMP, split_axis=0, concat_axis=0, tiled=True)
    size = lax.axis_size(CLUS_SAMP)
    ends = range(7, size - 1, 8)
    cross = lax.ppermute(own, CLUS_SAMP, [(i, i + 1) for i in ends] + [(i + 1, i) for i in ends])

    wa, wb, ua, ub = call(
        prep_kernel,
        [shape(32, 8, 8, 128), shape(32, 8, 8, 128), shape(32, 8, 128), shape(32, 8, 128)],
        [VMEM] * 4,
        [pltpu.SMEM((16, 256), ints), pltpu.SemaphoreType.DMA],
        flops=1 << 20, bytes_accessed=4 << 20,
    )(code, ta, tb, tab_up)

    payload = call(
        middle_kernel, shape(96, 4, 128), [VMEM] * 7, [pltpu.VMEM((8, 128), F32)],
        flops=4 << 20, bytes_accessed=3 << 20,
    )(gathered.reshape(192, 128), weights, wa, wb, ua, ub, rot)
    parts = lax.all_to_all(payload, CLUS, split_axis=0, concat_axis=0, tiled=True)

    near_field = call(
        near_kernel, shape(8, 2, 128), [VMEM, VMEM, HBM, HBM, HBM],
        [
            pltpu.VMEM((8, 8, 2, 128, 128), F32),
            pltpu.VMEM((48, 128), F32),
            pltpu.VMEM((2, 256, 256), BF16),
            pltpu.SMEM((8, 8), ints),
            pltpu.SMEM((8,), ints),
            pltpu.SemaphoreType.DMA((10,)),
        ],
        flops=16 << 20, bytes_accessed=8 << 20,
    )(gathered, cross, neighbours, near_count, near_blocks)

    incoming_lower, incoming_upper = call(
        final_kernel, [shape(1, 2, 2, 256), shape(1, 2, 2, 96)], [VMEM],
        flops=1 << 17, bytes_accessed=1 << 18,
    )(parts)
    return near_field, incoming_lower, incoming_upper


def solution(mesh):
    split = Mesh(mesh.devices.reshape(4, 8, 4, 2), CLUS_SAMP)
    whole = P()
    return jax.shard_map(
        local,
        mesh=split,
        in_specs=(
            P(CLUS_SAMP), P(CLUS_SAMP), P(CLUS_SAMP), P(CLUS_SAMP), P(CLUS_SAMP),
            whole, whole, P(None, SAMP), P(None, SAMP),
            whole, whole, whole, whole, P(None, None, SAMP), whole, whole, whole,
        ),
        out_specs=(P(CLUS_SAMP), P(CLUS_SAMP), P(CLUS, None, None, SAMP)),
        check_vma=False,
    )
```

time: 40.7 us -> 41.9 us (1.029)
  the two profiles are of different devices: /device:TPU:32 before, /device:TPU:8 now
where the time goes in v4:
time: 41.9 us; the launch traced here: 41.5 us
  starting transfers between devices  19.9 us (47%)
  Pallas kernels  11.1 us (26%)
  waiting for transfers between devices  9.81 us (23%)
  between operations  0.69 us (2%)
    all_to_all x1, starting transfers between devices, local(): lax.all_to_all(payload, CLUS, split_axis=0, concat_axis=0, tiled=True)  11.7 us
    pallas_call x5, Pallas kernels, placed(): run(*(x if spec is VMEM else pltpu.with_memory_space_constraint(x, spec.m...  11.1 us
    ppermute x1, waiting for transfers between devices, local(): lax.ppermute(own, CLUS_SAMP, [(i, i + 1) for i in ends] + [(i + 1, i) for...  5.53 us
    all_to_all x1, starting transfers between devices, local(): lax.all_to_all(message, SAMP, split_axis=0, concat_axis=0, tiled=True)  4.31 us
    all_to_all x1, waiting for transfers between devices, local(): lax.all_to_all(message, SAMP, split_axis=0, concat_axis=0, tiled=True)  4.27 us
    ppermute x1, starting transfers between devices, local(): lax.ppermute(own, CLUS_SAMP, [(i, i + 1) for i in ends] + [(i + 1, i) for...  3.92 us
  transfers between devices with their start and end apart: 3, of which 2 were waited for; matrix products, arithmetic and copies ran while one was open for 0% of the time, Pallas kernels for 15%

profile of v4, /device:TPU:8, one launch (start us, length us, event | category | flops | bytes accessed | tf_op | source)
XLA Modules:
  0.0 41.5 jit_solution(3297072150968206614)
XLA Ops:
  0.6 3.3 %shard_map.184 = (f32[8,24,128]{2,1,0:T(8,128)}, s32[16,256]{1,0:T(8,128)S(1)}, f32[65,8,128]{2,1,0:T(8,128)S(1)}, f32[65,8,128]{2,1,0:T(8,128)S(1)}, f32[64,2,9...) custom-call(f32[8,2,128]{2,1,0:T(2,128)} %cur_h.1, f32[8,2,2,128,128]{4,3,2,1,0:T(8,128)} %rad_h.1, ...), custom_call_target="tpu_custom_call" | custom-call | flops 4194304 | bytes 3145728 | tf_op jit(solution)/shard_map/pallas_call | solution.py:39
  3.9 4.3 %all-to-all-start = ((f32[8,24,128]{2,1,0:T(8,128)}), f32[8,24,128]{2,1,0:T(8,128)S(1)}, u32[]{:S(2)}, u32[]{:S(2)}) async-start(f32[8,24,128]{2,1,0:T(8,128)} %get-tuple-element.19), calls=%async_computation | async-start | bytes 196608 | tf_op jit(solution)/shard_map/all_to_all | solution.py:323
  8.3 1.5 %shard_map.186 = (f32[32,8,8,128]{3,2,1,0:T(8,128)S(1)}, f32[32,8,8,128]{3,2,1,0:T(8,128)S(1)}, f32[32,8,128]{2,1,0:T(8,128)S(1)}, f32[32,8,128]{2,1,0:T(8,128)S(1)}) custom-call(s32[16,256]{1,0:T(8,128)S(1)} %get-tuple-element.22.code_v, f32[65,8,128]{2,1,0:T(8,128)S(1)} %get-tuple-element.23.ta, f32[65,8,128]{2,1,0:T(8,128)S(1)} %get-tuple-element.24.tb, ...), custom_call_target="tpu_custom_call" | custom-call | flops 1048576 | bytes 4194304 | tf_op jit(solution)/shard_map/pallas_call | solution.py:39
  9.8 4.3 %all-to-all-done.got = f32[8,24,128]{2,1,0:T(8,128)S(1)} async-done(((f32[8,24,128]{2,1,0:T(8,128)}), f32[8,24,128]{2,1,0:T(8,128)S(1)}, u32[]{:S(2)}, u32[]{:S(2)}) %all-to-all-start) | async-done | bytes 98336 | tf_op jit(solution)/shard_map/all_to_all | solution.py:323
  14.1 0.9 %shard_map.187 = f32[96,4,128]{2,1,0:T(4,128)} custom-call(f32[192,128]{1,0:T(8,128)S(1)} %bitcast.8, bf16[96,768]{1,0:T(8,128)(2,1)S(1)} %get-tuple-element.21.weights, f32[32,8,8,128]{3,2,1,0:T(8,128)S(1)} %get-tuple-element.26.wa, f32[32,8,8,128]{3,2,1,0:T(8,128)S(1)} %get-tuple-element.27.wb, f32[32,8,128]{2,1,0:T(8,128)S(1)} %get-tuple-element.28.ua, ...), custom_call_target="tpu_custom_call" | custom-call | flops 4194304 | bytes 3145728 | tf_op jit(solution)/shard_map/pallas_call | solution.py:39
  15.0 11.7 %all-to-all-start.1 = ((f32[96,4,128]{2,1,0:T(4,128)}), f32[96,4,128]{2,1,0:T(4,128)S(1)}, u32[]{:S(2)}, u32[]{:S(2)}) async-start(f32[96,4,128]{2,1,0:T(4,128)} %shard_map.187), calls=%async_computation.1 | async-start | bytes 393216 | tf_op jit(solution)/shard_map/all_to_all | solution.py:340
  26.7 3.9 %collective-permute-start = (f32[8,2,128]{2,1,0:T(2,128)}, f32[8,2,128]{2,1,0:T(2,128)S(1)}, u32[]{:S(2)}, u32[]{:S(2)}) collective-permute-start(f32[8,2,128]{2,1,0:T(2,128)} %cur_h.1), channel_id=1, source_target_pairs={{7,8},{15,16},{23,24},{31,32},{39,40},{47,48},{55,56},{63,64},{71,... | collective-permute-start | bytes 24584 | tf_op jit(solution)/shard_map/ppermute | solution.py:326
  30.6 5.5 %collective-permute-done.cross = f32[8,2,128]{2,1,0:T(2,128)S(1)} collective-permute-done((f32[8,2,128]{2,1,0:T(2,128)}, f32[8,2,128]{2,1,0:T(2,128)S(1)}, u32[]{:S(2)}, u32[]{:S(2)}) %collective-permute-start) | collective-permute-done | bytes 8224 | tf_op jit(solution)/shard_map/ppermute | solution.py:326
  36.2 4.7 %shard_map.185 = f32[8,2,128]{2,1,0:T(2,128)} custom-call(f32[8,24,128]{2,1,0:T(8,128)S(1)} %all-to-all-done.got, f32[8,2,128]{2,1,0:T(2,128)S(1)} %collective-permute-done.cross, s32[8,8]{1,0:T(8,128)} %neighbours_h.1, s32[8]{0:T(128)} %count_h.1, f32[8,8,2,128,128]{4,3,2,1,0:T(8,128)} %blocks_h.1), custom_call_target="tpu_custom_call" | custom-call | flops 16777216 | bytes 8388608 | tf_op jit(solution)/shard_map/pallas_call | solution.py:39
  40.8 0.0 all-to-all-done.1.got
  40.9 0.6 %shard_map.188 = (f32[1,2,2,256]{3,2,1,0:T(2,128)}, f32[1,2,2,96]{3,2,1,0:T(2,128)}) custom-call(f32[96,4,128]{2,1,0:T(4,128)S(1)} %all-to-all-done.1.got), custom_call_target="tpu_custom_call" | custom-call | flops 131072 | bytes 262144 | tf_op jit(solution)/shard_map/pallas_call | solution.py:39
Async XLA Ops:
  3.9 10.1 %all-to-all-start = ((f32[8,24,128]{2,1,0:T(8,128)}), f32[8,24,128]{2,1,0:T(8,128)S(1)}, u32[]{:S(2)}, u32[]{:S(2)}) async-start(f32[8,24,128]{2,1,0:T(8,128)} %get-tuple-element.19), calls=%async_computation | async-start | bytes 196608 | tf_op jit(solution)/shard_map/all_to_all | solution.py:323
  15.0 25.8 %all-to-all-start.1 = ((f32[96,4,128]{2,1,0:T(4,128)}), f32[96,4,128]{2,1,0:T(4,128)S(1)}, u32[]{:S(2)}, u32[]{:S(2)}) async-start(f32[96,4,128]{2,1,0:T(4,128)} %shard_map.187), calls=%async_computation.1 | async-start | bytes 393216 | tf_op jit(solution)/shard_map/all_to_all | solution.py:340
  26.7 9.5 %collective-permute-start = (f32[8,2,128]{2,1,0:T(2,128)}, f32[8,2,128]{2,1,0:T(2,128)S(1)}, u32[]{:S(2)}, u32[]{:S(2)}) collective-permute-start(f32[8,2,128]{2,1,0:T(2,128)} %cur_h.1), channel_id=1, source_target_pairs={{7,8},{15,16},{23,24},{31,32},{39,40},{47,48},{55,56},{63,64},{71,... | collective-permute-start | bytes 24584 | tf_op jit(solution)/shard_map/ppermute | solution.py:326

commit v5 on v4

--- a/solution.py
+++ b/solution.py
@@ -11,6 +11,7 @@
 CLUS_SAMP = CLUS + SAMP
 
 F32 = jnp.float32
+CHUNKS = 4
 BF16 = jnp.bfloat16
 VMEM = pl.BlockSpec(memory_space=pltpu.VMEM)
 SMEM = pl.BlockSpec(memory_space=pltpu.SMEM)
@@ -23,13 +24,13 @@
     return clus, samp
 
 
-def call(kernel, outs, in_specs, scratch=(), mib=16, flops=0, bytes_accessed=0):
+def call(kernel, outs, in_specs, scratch=(), mib=16, flops=0, bytes_accessed=0, first=None):
     many = isinstance(outs, (list, tuple))
     run = pl.pallas_call(
         kernel,
         out_shape=outs,
         in_specs=in_specs,
-        out_specs=[VMEM] * len(outs) if many else VMEM,
+        out_specs=[first or VMEM] + [VMEM] * (len(outs) - 1) if many else first or VMEM,
         scratch_shapes=list(scratch),
         compiler_params=pltpu.CompilerParams(vmem_limit_bytes=mib << 20),
         cost_estimate=pl.CostEstimate(flops=flops, bytes_accessed=bytes_accessed, transcendentals=0),
@@ -71,28 +72,72 @@
 
 
 def leaf_kernel(
-    cur_h, rad_h, interp_h, phase_h, src_low_h, op_low_h, cnt_low_h, src_up_h, op_up_h, cnt_up_h,
-    tab_low_h, tab_up_h, phase_up_h, interp_up_h,
-    out, code_v, ta, tb, tab_up, rot, weights,
-    cur, rad, interp, phase, src_low, op_low, cnt_low, src_up, op_up, cnt_up, tab_low, phase_up, interp_up,
-    pat, msg, sems,
+    cur_h, rad_h, interp_h, phase_h, in0, in1, in2, in3, in4, in5, in6, in7, in8, in9,
+    out, to0, to1, to2, to3, to4, to5, to6, to7, to8, to9,
+    cur, rad, interp, phase, pat, msg, sems, later_sems,
 ):
-    clus, _ = place()
-    copies = start_all(
-        [
-            (src_low_h, src_low), (op_low_h, op_low), (cnt_low_h, cnt_low), (src_up_h, src_up),
-            (op_up_h, op_up), (cnt_up_h, cnt_up), (cur_h, cur), (phase_h, phase), (interp_h, interp),
-            (tab_low_h, tab_low), (tab_up_h, tab_up), (phase_up_h, phase_up), (interp_up_h, interp_up),
-        ]
-        + [(rad_h.at[b], rad.at[b]) for b in range(8)],
-        sems,
-    )
-    for copy in copies[:13]:
+    later_h = [in0, in1, in2, in3, in4, in5, in6, in7, in8, in9]
+    later = [to0, to1, to2, to3, to4, to5, to6, to7, to8, to9]
+    chunk = 8 // CHUNKS
+    spans = [pl.ds(chunk * i, chunk) for i in range(CHUNKS)]
+    pairs = [(cur_h, cur)] + [(rad_h.at[span], rad.at[span]) for span in spans]
+    copies = start_all(pairs + [(interp_h, interp), (phase_h, phase)], sems)
+    others = start_all(list(zip(later_h, later)), later_sems)
+    copies[0].wait()
+    own = cur[...].reshape(16, 128)
+    msg[pl.ds(8, 16), :] = own
+    sent = [
+        pltpu.make_async_copy(msg.at[pl.ds(8, 16)], out.at[peer, pl.ds(8, 16)], sems.at[21 + peer])
+        for peer in range(8)
+    ]
+    for copy in sent:
+        copy.start()
+    columns = own.T
+    for b in range(8):
+        if b % chunk == 0:
+            copies[1 + b // chunk].wait()
+        cr = jnp.broadcast_to(columns[:, 2 * b : 2 * b + 1], (128, 128))
+        ci = jnp.broadcast_to(columns[:, 2 * b + 1 : 2 * b + 2], (128, 128))
+        for p in range(2):
+            rr = rad[b, p, 0]
+            ri = rad[b, p, 1]
+            pat[pl.ds(16 * p + b, 1), :] = jnp.sum(rr * cr - ri * ci, axis=0, keepdims=True)
+            pat[pl.ds(16 * p + 8 + b, 1), :] = jnp.sum(rr * ci + ri * cr, axis=0, keepdims=True)
+    copies[-2].wait()
+    copies[-1].wait()
+    high, low = pieces_of(interp[...])
+    weights_leaf = jnp.concatenate([high, low, high], axis=0)
+    cosine = jnp.cos(phase[...])
+    sine = jnp.sin(phase[...])
+    high, low = pieces_of(pat[...])
+    lifted = jnp.dot(
+        jnp.concatenate([high, high, low], axis=1), weights_leaf, preferred_element_type=F32
+    )
+    for p in range(2):
+        for c, part in enumerate(rotated(cosine, sine, lifted, p)):
+            for h in range(2):
+                msg[pl.ds(4 * p + 2 * c + h, 1), :] = part[:, 128 * h : 128 * h + 128]
+    last = [
+        pltpu.make_async_copy(msg.at[pl.ds(0, 8)], out.at[peer, pl.ds(0, 8)], sems.at[29 + peer])
+        for peer in range(8)
+    ]
+    for copy in last:
+        copy.start()
+    for copy in others + sent + last:
         copy.wait()
+
+
+def prep_kernel(
+    src_low, op_low, cnt_low, src_up, op_up, cnt_up, tab_low, tab_up, phase_up, interp_up,
+    wa, wb, ua, ub, rot, weights, code_v, ta, tb, code_s, sem,
+):
+    clus, samp = place()
     zero = jnp.zeros((8, 128), F32)
     row = rows_of((8, 128), 0)
     first_half = (row & 1) == 0
     sign_low = jnp.where((row & 2) == 0, -1.0, 1.0).astype(F32)
+    sign_up = jnp.where((row & 1) == 0, -1.0, 1.0).astype(F32)[:, :96]
+    code_v[pl.ds(8, 8), :] = jnp.zeros((8, 256), jnp.int32)
     src = src_low[...]
     used = (rows_of(src.shape, 0) < cnt_low[...]) & ((src >> 3) == clus)
     code = 64 - op_low[...]
@@ -100,11 +145,16 @@
     for o in range(8):
         listed = jnp.sum(jnp.where(used & (octant == o), code, 0), axis=0, keepdims=True)
         code_v[pl.ds(o, 1), :] = 64 - listed
-    code_v[pl.ds(8, 8), :] = jnp.zeros((8, 256), jnp.int32)
     used_up = (rows_of(src_up.shape, 0) < cnt_up[...]) & (src_up[...] == clus)
     code_v[pl.ds(8, 1), pl.ds(0, 32)] = jnp.sum(jnp.where(used_up, op_up[...] + 1, 0), axis=0, keepdims=True)
+    move = pltpu.make_async_copy(code_v, code_s, sem)
+    move.start()
     ta[64] = zero
     tb[64] = zero
+    rot[0] = zero
+    rot[1] = zero
+    ua[...] = jnp.zeros((32, 8, 128), F32)
+    ub[...] = jnp.zeros((32, 8, 128), F32)
 
     def expand(n, carry):
         parts = []
@@ -117,50 +167,10 @@
         return carry
 
     lax.fori_loop(0, 64, expand, 0, unroll=8)
-    rot[0] = zero
-    rot[1] = zero
     rot[0, :, pl.ds(0, 96)] = jnp.cos(phase_up[...])
     rot[1, :, pl.ds(0, 96)] = jnp.sin(phase_up[...])
     high, low = pieces_of(interp_up[...])
     weights[...] = jnp.concatenate([high, low, high], axis=1)
-    high, low = pieces_of(interp[...])
-    weights_leaf = jnp.concatenate([high, low, high], axis=0)
-    cosine = jnp.cos(phase[...])
-    sine = jnp.sin(phase[...])
-    own = cur[...].reshape(16, 128)
-    for peer in range(8):
-        out[peer, pl.ds(8, 16), :] = own
-    columns = own.T
-    for b in range(8):
-        copies[13 + b].wait()
-        cr = jnp.broadcast_to(columns[:, 2 * b : 2 * b + 1], (128, 128))
-        ci = jnp.broadcast_to(columns[:, 2 * b + 1 : 2 * b + 2], (128, 128))
-        for p in range(2):
-            rr = rad[b, p, 0]
-            ri = rad[b, p, 1]
-            pat[pl.ds(16 * p + b, 1), :] = jnp.sum(rr * cr - ri * ci, axis=0, keepdims=True)
-            pat[pl.ds(16 * p + 8 + b, 1), :] = jnp.sum(rr * ci + ri * cr, axis=0, keepdims=True)
-    high, low = pieces_of(pat[...])
-    lifted = jnp.dot(
-        jnp.concatenate([high, high, low], axis=1), weights_leaf, preferred_element_type=F32
-    )
-    for p in range(2):
-        for c, part in enumerate(rotated(cosine, sine, lifted, p)):
-            for h in range(2):
-                msg[pl.ds(4 * p + 2 * c + h, 1), :] = part[:, 128 * h : 128 * h + 128]
-    whole = msg[...]
-    for peer in range(8):
-        out[peer, pl.ds(0, 8), :] = whole
-
-
-def prep_kernel(code_v, ta, tb, tab_up, wa, wb, ua, ub, code_s, sem):
-    _, samp = place()
-    move = pltpu.make_async_copy(code_v, code_s, sem)
-    move.start()
-    row = rows_of((8, 128), 0)
-    sign_up = jnp.where((row & 1) == 0, -1.0, 1.0).astype(F32)[:, :96]
-    ua[...] = jnp.zeros((32, 8, 128), F32)
-    ub[...] = jnp.zeros((32, 8, 128), F32)
     move.wait()
 
     def target(t, carry):
@@ -175,7 +185,7 @@
         ub[t, :, pl.ds(0, 96)] = jnp.broadcast_to(tab_up[n, pl.ds(1, 1), :], (8, 96)) * listed * sign_up
         return carry
 
-    lax.fori_loop(0, 32, target, 0, unroll=2)
+    lax.fori_loop(0, 32, target, 0, unroll=4)
 
 
 def middle_kernel(got, weights, wa, wb, ua, ub, rot, out, upper):
@@ -297,22 +307,19 @@
     tables_upper, operator_upper, sources_upper, count_upper,
 ):
     ints = jnp.int32
-    message, code, ta, tb, tab_up, rot, weights = call(
-        leaf_kernel,
-        [
-            shape(8, 24, 128), jax.ShapeDtypeStruct((16, 256), ints), shape(65, 8, 128), shape(65, 8, 128),
-            shape(64, 2, 96), shape(2, 8, 128), jax.ShapeDtypeStruct((96, 768), BF16),
-        ],
-        [HBM] * 14,
+    ints = jnp.int32
+    kinds = [
+        ((16, 256), ints), ((16, 256), ints), ((1, 256), ints), ((7, 32), ints), ((7, 32), ints), ((1, 32), ints),
+        ((64, 2, 256), F32), ((64, 2, 96), F32), ((8, 96), F32), ((96, 256), F32),
+    ]
+    message, *lists = call(
+        leaf_kernel, [shape(8, 24, 128)] + [jax.ShapeDtypeStruct(*kind) for kind in kinds], [HBM] * 14,
         [
             pltpu.VMEM((8, 2, 128), F32), pltpu.VMEM((8, 2, 2, 128, 128), F32),
-            pltpu.VMEM((128, 256), F32), pltpu.VMEM((8, 256), F32),
-            pltpu.VMEM((16, 256), ints), pltpu.VMEM((16, 256), ints), pltpu.VMEM((1, 256), ints),
-            pltpu.VMEM((7, 32), ints), pltpu.VMEM((7, 32), ints), pltpu.VMEM((1, 32), ints),
-            pltpu.VMEM((64, 2, 256), F32), pltpu.VMEM((8, 96), F32), pltpu.VMEM((96, 256), F32),
-            pltpu.VMEM((32, 128), F32), pltpu.VMEM((8, 128), F32), pltpu.SemaphoreType.DMA((21,)),
+            pltpu.VMEM((128, 256), F32), pltpu.VMEM((8, 256), F32), pltpu.VMEM((32, 128), F32),
+            pltpu.VMEM((24, 128), F32), pltpu.SemaphoreType.DMA((37,)), pltpu.SemaphoreType.DMA((10,)),
         ],
-        flops=4 << 20, bytes_accessed=3 << 20,
+        flops=4 << 20, bytes_accessed=3 << 20, first=HBM,
     )(
         currents, radiation, interp_leaf, phase_leaf,
         sources_lower.T, operator_lower.T, count_lower.reshape(1, -1),
@@ -325,13 +332,19 @@
     ends = range(7, size - 1, 8)
     cross = lax.ppermute(own, CLUS_SAMP, [(i, i + 1) for i in ends] + [(i + 1, i) for i in ends])
 
-    wa, wb, ua, ub = call(
+    wa, wb, ua, ub, rot, weights = call(
         prep_kernel,
-        [shape(32, 8, 8, 128), shape(32, 8, 8, 128), shape(32, 8, 128), shape(32, 8, 128)],
-        [VMEM] * 4,
-        [pltpu.SMEM((16, 256), ints), pltpu.SemaphoreType.DMA],
+        [
+            shape(32, 8, 8, 128), shape(32, 8, 8, 128), shape(32, 8, 128), shape(32, 8, 128),
+            shape(2, 8, 128), jax.ShapeDtypeStruct((96, 768), BF16),
+        ],
+        [VMEM] * 10,
+        [
+            pltpu.VMEM((16, 256), ints), pltpu.VMEM((65, 8, 128), F32), pltpu.VMEM((65, 8, 128), F32),
+            pltpu.SMEM((16, 256), ints), pltpu.SemaphoreType.DMA,
+        ],
         flops=1 << 20, bytes_accessed=4 << 20,
-    )(code, ta, tb, tab_up)
+    )(*lists)
 
     payload = call(
         middle_kernel, shape(96, 4, 128), [VMEM] * 7, [pltpu.VMEM((8, 128), F32)],

time: 41.9 us -> 41.5 us (level)
  no operation moved by 1% of the time
where the time goes in v5:
time: 41.5 us; the launch traced here: 41.2 us
  starting transfers between devices  19.9 us (48%)
  Pallas kernels  10.8 us (26%)
  waiting for transfers between devices  9.83 us (24%)
  between operations  0.69 us (2%)
    all_to_all x1, starting transfers between devices, local(): lax.all_to_all(payload, CLUS, split_axis=0, concat_axis=0, tiled=True)  11.7 us
    pallas_call x5, Pallas kernels, placed(): run(*(x if spec is VMEM else pltpu.with_memory_space_constraint(x, spec.m...  10.8 us
    ppermute x1, waiting for transfers between devices, local(): lax.ppermute(own, CLUS_SAMP, [(i, i + 1) for i in ends] + [(i + 1, i) for...  5.53 us
    all_to_all x1, starting transfers between devices, local(): lax.all_to_all(message, SAMP, split_axis=0, concat_axis=0, tiled=True)  4.31 us
    all_to_all x1, waiting for transfers between devices, local(): lax.all_to_all(message, SAMP, split_axis=0, concat_axis=0, tiled=True)  4.3 us
    ppermute x1, starting transfers between devices, local(): lax.ppermute(own, CLUS_SAMP, [(i, i + 1) for i in ends] + [(i + 1, i) for...  3.92 us
  transfers between devices with their start and end apart: 3, of which 2 were waited for; matrix products, arithmetic and copies ran while one was open for 0% of the time, Pallas kernels for 15%

profile of v5, /device:TPU:8, one launch (start us, length us, event | category | flops | bytes accessed | tf_op | source)
XLA Modules:
  0.0 41.2 jit_solution(13163422020337627875)
XLA Ops:
  0.6 3.0 %shard_map.184 = (f32[8,24,128]{2,1,0:T(8,128)}, s32[16,256]{1,0:T(8,128)S(1)}, s32[16,256]{1,0:T(8,128)S(1)}, s32[1,256]{1,0:T(1,128)S(1)}, s32[7,32]{1,0:T(8,1...) custom-call(f32[8,2,128]{2,1,0:T(2,128)} %cur_h.1, ...), custom_call_target="tpu_custom_call" | custom-call | flops 4194304 | bytes 3145728 | tf_op jit(solution)/shard_map/pallas_call | solution.py:40
  3.7 4.3 %all-to-all-start = ((f32[8,24,128]{2,1,0:T(8,128)}), f32[8,24,128]{2,1,0:T(8,128)S(1)}, u32[]{:S(2)}, u32[]{:S(2)}) async-start(f32[8,24,128]{2,1,0:T(8,128)} %get-tuple-element.25), calls=%async_computation | async-start | bytes 196608 | tf_op jit(solution)/shard_map/all_to_all | solution.py:330
  8.0 1.5 %shard_map.186 = (f32[32,8,8,128]{3,2,1,0:T(8,128)S(1)}, f32[32,8,8,128]{3,2,1,0:T(8,128)S(1)}, f32[32,8,128]{2,1,0:T(8,128)S(1)}, f32[32,8,128]{2,1,0:T(8,128)S...) custom-call(s32[16,256]{1,0:T(8,128)S(1)} %get-tuple-element.27.src_low, ...), custom_call_target="tpu_custom_call" | custom-call | flops 1048576 | bytes 4194304 | tf_op jit(solution)/shard_map/pallas_call | solution.py:40
  9.5 4.3 %all-to-all-done.got = f32[8,24,128]{2,1,0:T(8,128)S(1)} async-done(((f32[8,24,128]{2,1,0:T(8,128)}), f32[8,24,128]{2,1,0:T(8,128)S(1)}, u32[]{:S(2)}, u32[]{:S(2)}) %all-to-all-start) | async-done | bytes 98336 | tf_op jit(solution)/shard_map/all_to_all | solution.py:330
  13.8 0.9 %shard_map.187 = f32[96,4,128]{2,1,0:T(4,128)} custom-call(f32[192,128]{1,0:T(8,128)S(1)} %bitcast.8, bf16[96,768]{1,0:T(8,128)(2,1)S(1)} %get-tuple-element.37.weights, f32[32,8,8,128]{3,2,1,0:T(8,128)S(1)} %get-tuple-element.38.wa, f32[32,8,8,128]{3,2,1,0:T(8,128)S(1)} %get-tuple-element.39.wb, f32[32,8,128]{2,1,0:T(8,128)S(1)} %get-tuple-element.40.ua, ...), custom_call_target="tpu_custom_call" | custom-call | flops 4194304 | bytes 3145728 | tf_op jit(solution)/shard_map/pallas_call | solution.py:40
  14.7 11.7 %all-to-all-start.1 = ((f32[96,4,128]{2,1,0:T(4,128)}), f32[96,4,128]{2,1,0:T(4,128)S(1)}, u32[]{:S(2)}, u32[]{:S(2)}) async-start(f32[96,4,128]{2,1,0:T(4,128)} %shard_map.187), calls=%async_computation.1 | async-start | bytes 393216 | tf_op jit(solution)/shard_map/all_to_all | solution.py:353
  26.4 3.9 %collective-permute-start = (f32[8,2,128]{2,1,0:T(2,128)}, f32[8,2,128]{2,1,0:T(2,128)S(1)}, u32[]{:S(2)}, u32[]{:S(2)}) collective-permute-start(f32[8,2,128]{2,1,0:T(2,128)} %cur_h.1), channel_id=1, source_target_pairs={{7,8},{15,16},{23,24},{31,32},{39,40},{47,48},{55,56},{63,64},{71,... | collective-permute-start | bytes 24584 | tf_op jit(solution)/shard_map/ppermute | solution.py:333
  30.4 5.5 %collective-permute-done.cross = f32[8,2,128]{2,1,0:T(2,128)S(1)} collective-permute-done((f32[8,2,128]{2,1,0:T(2,128)}, f32[8,2,128]{2,1,0:T(2,128)S(1)}, u32[]{:S(2)}, u32[]{:S(2)}) %collective-permute-start) | collective-permute-done | bytes 8224 | tf_op jit(solution)/shard_map/ppermute | solution.py:333
  35.9 4.7 %shard_map.185 = f32[8,2,128]{2,1,0:T(2,128)} custom-call(f32[8,24,128]{2,1,0:T(8,128)S(1)} %all-to-all-done.got, f32[8,2,128]{2,1,0:T(2,128)S(1)} %collective-permute-done.cross, s32[8,8]{1,0:T(8,128)} %neighbours_h.1, s32[8]{0:T(128)} %count_h.1, f32[8,8,2,128,128]{4,3,2,1,0:T(8,128)} %blocks_h.1), custom_call_target="tpu_custom_call" | custom-call | flops 16777216 | bytes 8388608 | tf_op jit(solution)/shard_map/pallas_call | solution.py:40
  40.6 0.0 all-to-all-done.1.got
  40.6 0.6 %shard_map.188 = (f32[1,2,2,256]{3,2,1,0:T(2,128)}, f32[1,2,2,96]{3,2,1,0:T(2,128)}) custom-call(f32[96,4,128]{2,1,0:T(4,128)S(1)} %all-to-all-done.1.got), custom_call_target="tpu_custom_call" | custom-call | flops 131072 | bytes 262144 | tf_op jit(solution)/shard_map/pallas_call | solution.py:40
Async XLA Ops:
  3.7 10.1 %all-to-all-start = ((f32[8,24,128]{2,1,0:T(8,128)}), f32[8,24,128]{2,1,0:T(8,128)S(1)}, u32[]{:S(2)}, u32[]{:S(2)}) async-start(f32[8,24,128]{2,1,0:T(8,128)} %get-tuple-element.25), calls=%async_computation | async-start | bytes 196608 | tf_op jit(solution)/shard_map/all_to_all | solution.py:330
  14.7 25.8 %all-to-all-start.1 = ((f32[96,4,128]{2,1,0:T(4,128)}), f32[96,4,128]{2,1,0:T(4,128)S(1)}, u32[]{:S(2)}, u32[]{:S(2)}) async-start(f32[96,4,128]{2,1,0:T(4,128)} %shard_map.187), calls=%async_computation.1 | async-start | bytes 393216 | tf_op jit(solution)/shard_map/all_to_all | solution.py:353
  26.4 9.5 %collective-permute-start = (f32[8,2,128]{2,1,0:T(2,128)}, f32[8,2,128]{2,1,0:T(2,128)S(1)}, u32[]{:S(2)}, u32[]{:S(2)}) collective-permute-start(f32[8,2,128]{2,1,0:T(2,128)} %cur_h.1), channel_id=1, source_target_pairs={{7,8},{15,16},{23,24},{31,32},{39,40},{47,48},{55,56},{63,64},{71,... | collective-permute-start | bytes 24584 | tf_op jit(solution)/shard_map/ppermute | solution.py:333

commit v6 on v5

--- a/solution.py
+++ b/solution.py
@@ -9,6 +9,7 @@
 CLUS = ("clus_0", "clus_1")
 SAMP = ("samp_0", "samp_1")
 CLUS_SAMP = CLUS + SAMP
+LAYER = ("clus_0",) + SAMP
 
 F32 = jnp.float32
 CHUNKS = 4
@@ -19,18 +20,16 @@
 
 
 def place():
-    clus = lax.axis_index("clus_0") * 8 + lax.axis_index("clus_1")
-    samp = lax.axis_index("samp_0") * 2 + lax.axis_index("samp_1")
-    return clus, samp
-
-
-def call(kernel, outs, in_specs, scratch=(), mib=16, flops=0, bytes_accessed=0, first=None):
+    return lax.axis_index("clus_0"), lax.axis_index("clus_1"), lax.axis_index("samp_0") * 2 + lax.axis_index("samp_1")
+
+
+def call(kernel, outs, in_specs, scratch=(), mib=16, flops=0, bytes_accessed=0):
     many = isinstance(outs, (list, tuple))
     run = pl.pallas_call(
         kernel,
         out_shape=outs,
         in_specs=in_specs,
-        out_specs=[first or VMEM] + [VMEM] * (len(outs) - 1) if many else first or VMEM,
+        out_specs=[VMEM] * len(outs) if many else VMEM,
         scratch_shapes=list(scratch),
         compiler_params=pltpu.CompilerParams(vmem_limit_bytes=mib << 20),
         cost_estimate=pl.CostEstimate(flops=flops, bytes_accessed=bytes_accessed, transcendentals=0),
@@ -84,15 +83,7 @@
     copies = start_all(pairs + [(interp_h, interp), (phase_h, phase)], sems)
     others = start_all(list(zip(later_h, later)), later_sems)
     copies[0].wait()
-    own = cur[...].reshape(16, 128)
-    msg[pl.ds(8, 16), :] = own
-    sent = [
-        pltpu.make_async_copy(msg.at[pl.ds(8, 16)], out.at[peer, pl.ds(8, 16)], sems.at[21 + peer])
-        for peer in range(8)
-    ]
-    for copy in sent:
-        copy.start()
-    columns = own.T
+    columns = cur[...].reshape(16, 128).T
     for b in range(8):
         if b % chunk == 0:
             copies[1 + b // chunk].wait()
@@ -117,13 +108,10 @@
         for c, part in enumerate(rotated(cosine, sine, lifted, p)):
             for h in range(2):
                 msg[pl.ds(4 * p + 2 * c + h, 1), :] = part[:, 128 * h : 128 * h + 128]
-    last = [
-        pltpu.make_async_copy(msg.at[pl.ds(0, 8)], out.at[peer, pl.ds(0, 8)], sems.at[29 + peer])
-        for peer in range(8)
-    ]
-    for copy in last:
-        copy.start()
-    for copy in others + sent + last:
+    whole = msg[...]
+    for peer in range(32):
+        out[peer] = whole
+    for copy in others:
         copy.wait()
 
 
@@ -131,30 +119,32 @@
     src_low, op_low, cnt_low, src_up, op_up, cnt_up, tab_low, tab_up, phase_up, interp_up,
     wa, wb, ua, ub, rot, weights, code_v, ta, tb, code_s, sem,
 ):
-    clus, samp = place()
+    y, z, samp = place()
     zero = jnp.zeros((8, 128), F32)
     row = rows_of((8, 128), 0)
     first_half = (row & 1) == 0
     sign_low = jnp.where((row & 2) == 0, -1.0, 1.0).astype(F32)
     sign_up = jnp.where((row & 1) == 0, -1.0, 1.0).astype(F32)[:, :96]
-    code_v[pl.ds(8, 8), :] = jnp.zeros((8, 256), jnp.int32)
     src = src_low[...]
-    used = (rows_of(src.shape, 0) < cnt_low[...]) & ((src >> 3) == clus)
-    code = 64 - op_low[...]
-    octant = src & 7
-    for o in range(8):
-        listed = jnp.sum(jnp.where(used & (octant == o), code, 0), axis=0, keepdims=True)
-        code_v[pl.ds(o, 1), :] = 64 - listed
-    used_up = (rows_of(src_up.shape, 0) < cnt_up[...]) & (src_up[...] == clus)
-    code_v[pl.ds(8, 1), pl.ds(0, 32)] = jnp.sum(jnp.where(used_up, op_up[...] + 1, 0), axis=0, keepdims=True)
+    used = rows_of(src.shape, 0) < cnt_low[...]
+    code = jnp.where(used, 64 - op_low[...], 0)
+    for g in range(32):
+        box = 64 * (g // 8) + 8 * z + g % 8
+        listed = jnp.sum(jnp.where(src == box, code, 0), axis=0, keepdims=True)
+        code_v[pl.ds(g, 1), :] = 64 - listed
+    code_v[pl.ds(32, 8), :] = jnp.zeros((8, 256), jnp.int32)
+    used_up = rows_of(src_up.shape, 0) < cnt_up[...]
+    for k in range(4):
+        mine = used_up & (src_up[...] == 8 * k + z)
+        code_v[pl.ds(32 + k, 1), pl.ds(0, 32)] = jnp.sum(jnp.where(mine, op_up[...] + 1, 0), axis=0, keepdims=True)
     move = pltpu.make_async_copy(code_v, code_s, sem)
     move.start()
     ta[64] = zero
     tb[64] = zero
     rot[0] = zero
     rot[1] = zero
-    ua[...] = jnp.zeros((32, 8, 128), F32)
-    ub[...] = jnp.zeros((32, 8, 128), F32)
+    ua[...] = jnp.zeros((8, 4, 8, 128), F32)
+    ub[...] = jnp.zeros((8, 4, 8, 128), F32)
 
     def expand(n, carry):
         parts = []
@@ -174,74 +164,84 @@
     move.wait()
 
     def target(t, carry):
-        for o in range(8):
-            n = code_s[o, t * 8 + samp]
-            wa[t, o] = ta[n]
-            wb[t, o] = tb[n]
-        i = code_s[8, t]
-        n = jnp.maximum(i - 1, 0)
-        listed = jnp.where(i > 0, 1.0, 0.0).astype(F32)
-        ua[t, :, pl.ds(0, 96)] = jnp.broadcast_to(tab_up[n, pl.ds(0, 1), :], (8, 96)) * listed
-        ub[t, :, pl.ds(0, 96)] = jnp.broadcast_to(tab_up[n, pl.ds(1, 1), :], (8, 96)) * listed * sign_up
+        clus = 8 * y + t
+        for g in range(32):
+            n = code_s[g, 8 * clus + samp]
+            wa[t, g] = ta[n]
+            wb[t, g] = tb[n]
+        for k in range(4):
+            i = code_s[32 + k, clus]
+            n = jnp.maximum(i - 1, 0)
+            listed = jnp.where(i > 0, 1.0, 0.0).astype(F32)
+            real = jnp.broadcast_to(tab_up[n, pl.ds(0, 1), :], (8, 96)) * listed
+            imag = jnp.broadcast_to(tab_up[n, pl.ds(1, 1), :], (8, 96)) * listed
+            ua[t, k, :, pl.ds(0, 96)] = real
+            ub[t, k, :, pl.ds(0, 96)] = imag * sign_up
         return carry
 
-    lax.fori_loop(0, 32, target, 0, unroll=4)
+    lax.fori_loop(0, 8, target, 0)
 
 
 def middle_kernel(got, weights, wa, wb, ua, ub, rot, out, upper):
     row = rows_of((8, 128), 0)
     halves = []
     for h in range(2):
-        halves.append(
-            jnp.concatenate([got[pl.ds(2 * k + h, 8, stride=24), :] for k in range(4)], axis=0)
-        )
+        parts = [got[pl.ds(64 * y + 2 * k + h, 8, stride=8), :] for y in range(4) for k in range(4)]
+        halves.append(jnp.concatenate(parts, axis=0))
     high, low = pieces_of(jnp.concatenate(halves, axis=1))
     lifted = lax.dot_general(
         jnp.concatenate([high, high, low], axis=1), weights[...], (((1,), (1,)), ((), ())),
         preferred_element_type=F32,
     )
-    plain = [got[pl.ds(24 * o, 8), :] for o in range(8)]
-    swapped = [
-        jnp.where((row & 2) == 0, pltpu.roll(x, 6, 0), pltpu.roll(x, 2, 0)) for x in plain
-    ]
-    for t in range(32):
-        total = wa[t, 0] * plain[0] + wb[t, 0] * swapped[0]
-        for o in range(1, 8):
-            total += wa[t, o] * plain[o] + wb[t, o] * swapped[o]
-        out[3 * t] = total[:4]
-        out[3 * t + 1] = total[4:]
-    upper[...] = jnp.zeros((8, 128), F32)
+    totals = [None] * 8
+    for block in range(4):
+        plain = [got[pl.ds(64 * block + 8 * o, 8), :] for o in range(8)]
+        swapped = [
+            jnp.where((row & 2) == 0, pltpu.roll(x, 6, 0), pltpu.roll(x, 2, 0)) for x in plain
+        ]
+        for t in range(8):
+            for o in range(8):
+                g = 8 * block + o
+                term = wa[t, g] * plain[o] + wb[t, g] * swapped[o]
+                totals[t] = term if totals[t] is None else totals[t] + term
+    for t in range(8):
+        out[3 * t] = totals[t][:4]
+        out[3 * t + 1] = totals[t][4:]
+    upper[...] = jnp.zeros((4, 8, 128), F32)
     cosine = rot[0][:, :96]
     sine = rot[1][:, :96]
-    for p in range(2):
-        for c, part in enumerate(rotated(cosine, sine, lifted, p)):
-            upper[pl.ds(2 * p + c, 1), pl.ds(0, 96)] = part
-    up = upper[...]
-    up_swapped = jnp.where((row & 1) == 0, pltpu.roll(up, 7, 0), pltpu.roll(up, 1, 0))
-    for t in range(32):
-        out[3 * t + 2] = (ua[t] * up + ub[t] * up_swapped)[:4]
-
-
-def near_kernel(got, cross, neighbours_h, count_h, blocks_h, out, blocks, ext, pieces, neighbours, count, sems):
-    clus, samp = place()
-    base = (clus * 8 + samp) * 8 - 8
-    lists = start_all([(neighbours_h, neighbours), (count_h, count)], sems.at[pl.ds(8, 2)])
+    for y in range(4):
+        for p in range(2):
+            for c, part in enumerate(rotated(cosine, sine, lifted[32 * y : 32 * y + 32], p)):
+                upper[y, pl.ds(2 * p + c, 1), pl.ds(0, 96)] = part
+    ups = [upper[y] for y in range(4)]
+    pairs = [(up, jnp.where((row & 1) == 0, pltpu.roll(up, 7, 0), pltpu.roll(up, 1, 0))) for up in ups]
+    for t in range(8):
+        total = None
+        for y, (up, up_swapped) in enumerate(pairs):
+            term = ua[t, y] * up + ub[t, y] * up_swapped
+            total = term if total is None else total + term
+        out[3 * t + 2] = total[:4]
+
+
+def near_kernel(cur_h, even, odd, neighbours_h, count_h, blocks_h, out, cur, blocks, ext, pieces, neighbours, count, sems):
+    y, z, samp = place()
+    base = (64 * y + 8 * z + samp) * 8 - 8
+    lists = start_all([(cur_h, cur), (neighbours_h, neighbours), (count_h, count)], sems.at[pl.ds(8, 3)])
 
     def load(b):
         return pltpu.make_async_copy(blocks_h.at[b], blocks.at[b], sems.at[b])
 
     for b in range(8):
         load(b).start()
-    outside = cross[...].reshape(16, 128)
-    before = got[jnp.maximum(samp - 1, 0), pl.ds(8, 16), :]
-    after = got[jnp.minimum(samp + 1, 7), pl.ds(8, 16), :]
-    ext[pl.ds(0, 16), :] = jnp.where(samp > 0, before, outside)
-    ext[pl.ds(16, 16), :] = got[samp, pl.ds(8, 16), :]
-    ext[pl.ds(32, 16), :] = jnp.where(samp < 7, after, outside)
+    parity = samp & 1
+    ext[pl.ds(pl.multiple_of(32 * (1 - parity), 8), 16), :] = even[...].reshape(16, 128)
+    ext[pl.ds(pl.multiple_of(32 * parity, 8), 16), :] = odd[...].reshape(16, 128)
     pieces[...] = jnp.zeros((2, 256, 256), BF16)
     ones = jnp.ones((16, 256), BF16)
     for one in lists:
         one.wait()
+    ext[pl.ds(16, 16), :] = cur[...].reshape(16, 128)
 
     def finish(slot, b):
         summed = lax.dot_general(
@@ -286,7 +286,7 @@
 
 def final_kernel(got, out_low, out_up):
     sums = [got[k] for k in range(3)]
-    for t in range(1, 32):
+    for t in range(1, 8):
         for k in range(3):
             sums[k] += got[3 * t + k]
     for p in range(2):
@@ -313,13 +313,13 @@
         ((64, 2, 256), F32), ((64, 2, 96), F32), ((8, 96), F32), ((96, 256), F32),
     ]
     message, *lists = call(
-        leaf_kernel, [shape(8, 24, 128)] + [jax.ShapeDtypeStruct(*kind) for kind in kinds], [HBM] * 14,
+        leaf_kernel, [shape(32, 8, 128)] + [jax.ShapeDtypeStruct(*kind) for kind in kinds], [HBM] * 14,
         [
             pltpu.VMEM((8, 2, 128), F32), pltpu.VMEM((8, 2, 2, 128, 128), F32),
             pltpu.VMEM((128, 256), F32), pltpu.VMEM((8, 256), F32), pltpu.VMEM((32, 128), F32),
-            pltpu.VMEM((24, 128), F32), pltpu.SemaphoreType.DMA((37,)), pltpu.SemaphoreType.DMA((10,)),
+            pltpu.VMEM((8, 128), F32), pltpu.SemaphoreType.DMA((7,)), pltpu.SemaphoreType.DMA((10,)),
         ],
-        flops=4 << 20, bytes_accessed=3 << 20, first=HBM,
+        flops=4 << 20, bytes_accessed=3 << 20,
     )(
         currents, radiation, interp_leaf, phase_leaf,
         sources_lower.T, operator_lower.T, count_lower.reshape(1, -1),
@@ -327,43 +327,44 @@
         tables_lower, tables_upper, phase_upper, interp_upper.T,
     )
     own, message = lax.optimization_barrier((currents, message))
-    gathered = lax.all_to_all(message, SAMP, split_axis=0, concat_axis=0, tiled=True)
+    gathered = lax.all_to_all(message, LAYER, split_axis=0, concat_axis=0, tiled=True)
     size = lax.axis_size(CLUS_SAMP)
-    ends = range(7, size - 1, 8)
-    cross = lax.ppermute(own, CLUS_SAMP, [(i, i + 1) for i in ends] + [(i + 1, i) for i in ends])
+    even = lax.ppermute(own, CLUS_SAMP, [(i, i ^ 1) for i in range(size)])
+    odd = lax.ppermute(own, CLUS_SAMP, [(i, ((i + 1) ^ 1) - 1) for i in range(1, size - 1)])
 
     wa, wb, ua, ub, rot, weights = call(
         prep_kernel,
         [
-            shape(32, 8, 8, 128), shape(32, 8, 8, 128), shape(32, 8, 128), shape(32, 8, 128),
+            shape(8, 32, 8, 128), shape(8, 32, 8, 128), shape(8, 4, 8, 128), shape(8, 4, 8, 128),
             shape(2, 8, 128), jax.ShapeDtypeStruct((96, 768), BF16),
         ],
         [VMEM] * 10,
         [
-            pltpu.VMEM((16, 256), ints), pltpu.VMEM((65, 8, 128), F32), pltpu.VMEM((65, 8, 128), F32),
-            pltpu.SMEM((16, 256), ints), pltpu.SemaphoreType.DMA,
+            pltpu.VMEM((40, 256), ints), pltpu.VMEM((65, 8, 128), F32), pltpu.VMEM((65, 8, 128), F32),
+            pltpu.SMEM((40, 256), ints), pltpu.SemaphoreType.DMA,
         ],
         flops=1 << 20, bytes_accessed=4 << 20,
     )(*lists)
 
     payload = call(
-        middle_kernel, shape(96, 4, 128), [VMEM] * 7, [pltpu.VMEM((8, 128), F32)],
+        middle_kernel, shape(24, 4, 128), [VMEM] * 7, [pltpu.VMEM((4, 8, 128), F32)],
         flops=4 << 20, bytes_accessed=3 << 20,
-    )(gathered.reshape(192, 128), weights, wa, wb, ua, ub, rot)
-    parts = lax.all_to_all(payload, CLUS, split_axis=0, concat_axis=0, tiled=True)
+    )(gathered.reshape(256, 128), weights, wa, wb, ua, ub, rot)
+    parts = lax.all_to_all(payload, "clus_1", split_axis=0, concat_axis=0, tiled=True)
 
     near_field = call(
-        near_kernel, shape(8, 2, 128), [VMEM, VMEM, HBM, HBM, HBM],
+        near_kernel, shape(8, 2, 128), [HBM, VMEM, VMEM, HBM, HBM, HBM],
         [
+            pltpu.VMEM((8, 2, 128), F32),
             pltpu.VMEM((8, 8, 2, 128, 128), F32),
             pltpu.VMEM((48, 128), F32),
             pltpu.VMEM((2, 256, 256), BF16),
             pltpu.SMEM((8, 8), ints),
             pltpu.SMEM((8,), ints),
-            pltpu.SemaphoreType.DMA((10,)),
+            pltpu.SemaphoreType.DMA((11,)),
         ],
         flops=16 << 20, bytes_accessed=8 << 20,
-    )(gathered, cross, neighbours, near_count, near_blocks)
+    )(currents, even, odd, neighbours, near_count, near_blocks)
 
     incoming_lower, incoming_upper = call(
         final_kernel, [shape(1, 2, 2, 256), shape(1, 2, 2, 96)], [VMEM],

time: 41.5 us -> 42.1 us (1.014)
  starting transfers between devices: 19.9 us -> 22.8 us
  waiting for transfers between devices: 9.83 us -> 7.21 us
    ppermute x1 -> x2, waiting for transfers between devices: 5.53 us -> 2.57 us  [the longest x1 2.56 us: local(): lax.ppermute(own, CLUS_SAMP, [(i, (i + 1 ^ 1) - 1) for i in range(1, size...]
    ppermute x1 -> x2, starting transfers between devices: 3.92 us -> 6.82 us  [the longest x1 6.82 us: local(): lax.ppermute(own, CLUS_SAMP, [(i, (i + 1 ^ 1) - 1) for i in range(1, size...]
  transfers between devices with their start and end apart: 3 -> 4, of which waited for: 2 -> 2; matrix products, arithmetic and copies ran while one was open for 0% -> 0% of each run, Pallas kernels for 15% -> 16%
where the time goes in v6:
time: 42.1 us; the launch traced here: 41.7 us
  starting transfers between devices  22.8 us (54%)
  Pallas kernels  11 us (26%)
  waiting for transfers between devices  7.21 us (17%)
  between operations  0.7 us (2%)
    pallas_call x5, Pallas kernels, placed(): run(*(x if spec is VMEM else pltpu.with_memory_space_constraint(x, spec.m...  11 us
    all_to_all x1, starting transfers between devices, local(): lax.all_to_all(payload, 'clus_1', split_axis=0, concat_axis=0, tiled=True)  8.47 us
    all_to_all x1, starting transfers between devices, local(): lax.all_to_all(message, LAYER, split_axis=0, concat_axis=0, tiled=True)  7.55 us
    ppermute x1, starting transfers between devices, local(): lax.ppermute(own, CLUS_SAMP, [(i, (i + 1 ^ 1) - 1) for i in range(1, size...  6.82 us
    all_to_all x1, waiting for transfers between devices, local(): lax.all_to_all(message, LAYER, split_axis=0, concat_axis=0, tiled=True)  4.64 us
    ppermute x1, waiting for transfers between devices, local(): lax.ppermute(own, CLUS_SAMP, [(i, (i + 1 ^ 1) - 1) for i in range(1, size...  2.56 us
  transfers between devices with their start and end apart: 4, of which 2 were waited for; matrix products, arithmetic and copies ran while one was open for 0% of the time, Pallas kernels for 16%

profile of v6, /device:TPU:8, one launch (start us, length us, event | category | flops | bytes accessed | tf_op | source)
XLA Modules:
  0.0 41.7 jit_solution(17232815744991983433)
XLA Ops:
  0.6 2.8 %shard_map.184 = (f32[32,8,128]{2,1,0:T(8,128)}, s32[16,256]{1,0:T(8,128)S(1)}, s32[16,256]{1,0:T(8,128)S(1)}, s32[1,256]{1,0:T(1,128)S(1)}, s32[7,32]{1,0:T(8,1...) custom-call(f32[8,2,128]{2,1,0:T(2,128)} %cur_h.3, ...), custom_call_target="tpu_custom_call" | custom-call | flops 4194304 | bytes 3145728 | tf_op jit(solution)/shard_map/pallas_call | solution.py:39
  3.5 7.5 %all-to-all-start = ((f32[32,8,128]{2,1,0:T(8,128)}), f32[32,8,128]{2,1,0:T(8,128)S(1)}, u32[]{:S(2)}, u32[]{:S(2)}) async-start(f32[32,8,128]{2,1,0:T(8,128)} %get-tuple-element.26), calls=%async_computation | async-start | bytes 262144 | tf_op jit(solution)/shard_map/all_to_all | solution.py:330
  11.0 1.9 %shard_map.186 = (f32[8,32,8,128]{3,2,1,0:T(8,128)S(1)}, f32[8,32,8,128]{3,2,1,0:T(8,128)S(1)}, f32[8,4,8,128]{3,2,1,0:T(8,128)S(1)}, f32[8,4,8,128]{3,2,1,0:T(8...) custom-call(s32[16,256]{1,0:T(8,128)S(1)} %get-tuple-element.27.src_low, ...), custom_call_target="tpu_custom_call" | custom-call | flops 1048576 | bytes 4194304 | tf_op jit(solution)/shard_map/pallas_call | solution.py:39
  13.0 4.6 %all-to-all-done = f32[32,8,128]{2,1,0:T(8,128)S(1)} async-done(((f32[32,8,128]{2,1,0:T(8,128)}), f32[32,8,128]{2,1,0:T(8,128)S(1)}, u32[]{:S(2)}, u32[]{:S(2)}) %all-to-all-start) | async-done | bytes 131104 | tf_op jit(solution)/shard_map/all_to_all | solution.py:330
  17.6 1.0 %shard_map.187 = f32[24,4,128]{2,1,0:T(4,128)} custom-call(f32[256,128]{1,0:T(8,128)S(1)} %bitcast.8, bf16[96,768]{1,0:T(8,128)(2,1)S(1)} %get-tuple-element.37.weights, f32[8,32,8,128]{3,2,1,0:T(8,128)S(1)} %get-tuple-element.38.wa, f32[8,32,8,128]{3,2,1,0:T(8,128)S(1)} %get-tuple-element.39.wb, f32[8,4,8,128]{3,2,1,0:T(8,128)S(1)} %get-tuple-element.40.ua, ...), custom_call_target="tpu_custom_call" | custom-call | flops 4194304 | bytes 3145728 | tf_op jit(solution)/shard_map/pallas_call | solution.py:39
  18.6 8.5 %all-to-all-start.1 = ((f32[24,4,128]{2,1,0:T(4,128)}), f32[24,4,128]{2,1,0:T(4,128)S(1)}, u32[]{:S(2)}, u32[]{:S(2)}) async-start(f32[24,4,128]{2,1,0:T(4,128)} %shard_map.187), calls=%async_computation.1 | async-start | bytes 98304 | tf_op jit(solution)/shard_map/all_to_all | solution.py:353
  27.0 0.0 collective-permute-start
  27.0 6.8 %collective-permute-start.1 = (f32[8,2,128]{2,1,0:T(2,128)}, f32[8,2,128]{2,1,0:T(2,128)S(1)}, u32[]{:S(2)}, u32[]{:S(2)}) collective-permute-start(f32[8,2,128]{2,1,0:T(2,128)} %cur_h.3), channel_id=1, source_target_pairs={{1,2},{2,1},{3,4},{4,3},{5,6},{6,5},{7,8},{8,7},{9,10},{10,9},{11,... | collective-permute-start | bytes 24584 | tf_op jit(solution)/shard_map/ppermute | solution.py:333
  33.9 0.0 collective-permute-done.even
  33.9 2.6 %collective-permute-done.1.odd = f32[8,2,128]{2,1,0:T(2,128)S(1)} collective-permute-done((f32[8,2,128]{2,1,0:T(2,128)}, f32[8,2,128]{2,1,0:T(2,128)S(1)}, u32[]{:S(2)}, u32[]{:S(2)}) %collective-permute-start.1) | collective-permute-done | bytes 8224 | tf_op jit(solution)/shard_map/ppermute | solution.py:333
  36.4 4.7 %shard_map.185 = f32[8,2,128]{2,1,0:T(2,128)} custom-call(f32[8,2,128]{2,1,0:T(2,128)} %cur_h.3, f32[8,2,128]{2,1,0:T(2,128)S(1)} %collective-permute-done.even, f32[8,2,128]{2,1,0:T(2,128)S(1)} %collective-permute-done.1.odd, s32[8,8]{1,0:T(8,128)} %neighbours_h.1, s32[8]{0:T(128)} %count_h.1, f32[8,8,2,128,128]{4,3,2,1,0:T(8,128)} %blocks_h.1), custom_call_target="tpu_custom_call" | custom-call | flops 16777216 | bytes 8388608 | tf_op jit(solution)/shard_map/pallas_call | solution.py:39
  41.1 0.0 all-to-all-done.1.got
  41.1 0.6 %shard_map.188 = (f32[1,2,2,256]{3,2,1,0:T(2,128)}, f32[1,2,2,96]{3,2,1,0:T(2,128)}) custom-call(f32[24,4,128]{2,1,0:T(4,128)S(1)} %all-to-all-done.1.got), custom_call_target="tpu_custom_call" | custom-call | flops 131072 | bytes 262144 | tf_op jit(solution)/shard_map/pallas_call | solution.py:39
Async XLA Ops:
  3.5 14.1 %all-to-all-start = ((f32[32,8,128]{2,1,0:T(8,128)}), f32[32,8,128]{2,1,0:T(8,128)S(1)}, u32[]{:S(2)}, u32[]{:S(2)}) async-start(f32[32,8,128]{2,1,0:T(8,128)} %get-tuple-element.26), calls=%async_computation | async-start | bytes 262144 | tf_op jit(solution)/shard_map/all_to_all | solution.py:330
  18.6 22.6 %all-to-all-start.1 = ((f32[24,4,128]{2,1,0:T(4,128)}), f32[24,4,128]{2,1,0:T(4,128)S(1)}, u32[]{:S(2)}, u32[]{:S(2)}) async-start(f32[24,4,128]{2,1,0:T(4,128)} %shard_map.187), calls=%async_computation.1 | async-start | bytes 98304 | tf_op jit(solution)/shard_map/all_to_all | solution.py:353
  27.0 6.8 %collective-permute-start = (f32[8,2,128]{2,1,0:T(2,128)}, f32[8,2,128]{2,1,0:T(2,128)S(1)}, u32[]{:S(2)}, u32[]{:S(2)}) collective-permute-start(f32[8,2,128]{2,1,0:T(2,128)} %cur_h.3), channel_id=1, source_target_pairs={{0,1},{1,0},{2,3},{3,2},{4,5},{5,4},{6,7},{7,6},{8,9},{9,8},{10,11... | collective-permute-start | bytes 24584 | tf_op jit(solution)/shard_map/ppermute | solution.py:332
  27.0 9.4 %collective-permute-start.1 = (f32[8,2,128]{2,1,0:T(2,128)}, f32[8,2,128]{2,1,0:T(2,128)S(1)}, u32[]{:S(2)}, u32[]{:S(2)}) collective-permute-start(f32[8,2,128]{2,1,0:T(2,128)} %cur_h.3), channel_id=1, source_target_pairs={{1,2},{2,1},{3,4},{4,3},{5,6},{6,5},{7,8},{8,7},{9,10},{10,9},{11,... | collective-permute-start | bytes 24584 | tf_op jit(solution)/shard_map/ppermute | solution.py:333

commit v7 on v6

--- a/solution.py
+++ b/solution.py
@@ -71,12 +71,12 @@
 
 
 def leaf_kernel(
-    cur_h, rad_h, interp_h, phase_h, in0, in1, in2, in3, in4, in5, in6, in7, in8, in9,
-    out, to0, to1, to2, to3, to4, to5, to6, to7, to8, to9,
+    cur_h, rad_h, interp_h, phase_h, in0, in1, in2, in3, in4, in5,
+    out, to0, to1, to2, to3, to4, to5,
     cur, rad, interp, phase, pat, msg, sems, later_sems,
 ):
-    later_h = [in0, in1, in2, in3, in4, in5, in6, in7, in8, in9]
-    later = [to0, to1, to2, to3, to4, to5, to6, to7, to8, to9]
+    later_h = [in0, in1, in2, in3, in4, in5]
+    later = [to0, to1, to2, to3, to4, to5]
     chunk = 8 // CHUNKS
     spans = [pl.ds(chunk * i, chunk) for i in range(CHUNKS)]
     pairs = [(cur_h, cur)] + [(rad_h.at[span], rad.at[span]) for span in spans]
@@ -116,9 +116,12 @@
 
 
 def prep_kernel(
-    src_low, op_low, cnt_low, src_up, op_up, cnt_up, tab_low, tab_up, phase_up, interp_up,
-    wa, wb, ua, ub, rot, weights, code_v, ta, tb, code_s, sem,
+    src_low, op_low, cnt_low, src_up, op_up, cnt_up, tab_low_h, tab_up_h, phase_up_h, interp_up_h,
+    wa, wb, ua, ub, rot, weights, tab_low, tab_up, phase_up, interp_up, code_v, ta, tb, code_s, sem, sems,
 ):
+    copies = start_all(
+        [(tab_low_h, tab_low), (tab_up_h, tab_up), (phase_up_h, phase_up), (interp_up_h, interp_up)], sems
+    )
     y, z, samp = place()
     zero = jnp.zeros((8, 128), F32)
     row = rows_of((8, 128), 0)
@@ -145,6 +148,9 @@
     rot[1] = zero
     ua[...] = jnp.zeros((8, 4, 8, 128), F32)
     ub[...] = jnp.zeros((8, 4, 8, 128), F32)
+
+    for copy in copies:
+        copy.wait()
 
     def expand(n, carry):
         parts = []
@@ -310,21 +316,19 @@
     ints = jnp.int32
     kinds = [
         ((16, 256), ints), ((16, 256), ints), ((1, 256), ints), ((7, 32), ints), ((7, 32), ints), ((1, 32), ints),
-        ((64, 2, 256), F32), ((64, 2, 96), F32), ((8, 96), F32), ((96, 256), F32),
     ]
     message, *lists = call(
-        leaf_kernel, [shape(32, 8, 128)] + [jax.ShapeDtypeStruct(*kind) for kind in kinds], [HBM] * 14,
+        leaf_kernel, [shape(32, 8, 128)] + [jax.ShapeDtypeStruct(*kind) for kind in kinds], [HBM] * 10,
         [
             pltpu.VMEM((8, 2, 128), F32), pltpu.VMEM((8, 2, 2, 128, 128), F32),
             pltpu.VMEM((128, 256), F32), pltpu.VMEM((8, 256), F32), pltpu.VMEM((32, 128), F32),
-            pltpu.VMEM((8, 128), F32), pltpu.SemaphoreType.DMA((7,)), pltpu.SemaphoreType.DMA((10,)),
+            pltpu.VMEM((8, 128), F32), pltpu.SemaphoreType.DMA((7,)), pltpu.SemaphoreType.DMA((6,)),
         ],
         flops=4 << 20, bytes_accessed=3 << 20,
     )(
         currents, radiation, interp_leaf, phase_leaf,
         sources_lower.T, operator_lower.T, count_lower.reshape(1, -1),
         sources_upper.T, operator_upper.T, count_upper.reshape(1, -1),
-        tables_lower, tables_upper, phase_upper, interp_upper.T,
     )
     own, message = lax.optimization_barrier((currents, message))
     gathered = lax.all_to_all(message, LAYER, split_axis=0, concat_axis=0, tiled=True)
@@ -338,13 +342,14 @@
             shape(8, 32, 8, 128), shape(8, 32, 8, 128), shape(8, 4, 8, 128), shape(8, 4, 8, 128),
             shape(2, 8, 128), jax.ShapeDtypeStruct((96, 768), BF16),
         ],
-        [VMEM] * 10,
+        [VMEM] * 6 + [HBM] * 4,
         [
-            pltpu.VMEM((40, 256), ints), pltpu.VMEM((65, 8, 128), F32), pltpu.VMEM((65, 8, 128), F32),
-            pltpu.SMEM((40, 256), ints), pltpu.SemaphoreType.DMA,
+            pltpu.VMEM((64, 2, 256), F32), pltpu.VMEM((64, 2, 96), F32), pltpu.VMEM((8, 96), F32),
+            pltpu.VMEM((96, 256), F32), pltpu.VMEM((40, 256), ints), pltpu.VMEM((65, 8, 128), F32), pltpu.VMEM((65, 8, 128), F32),
+            pltpu.SMEM((40, 256), ints), pltpu.SemaphoreType.DMA, pltpu.SemaphoreType.DMA((4,)),
         ],
         flops=1 << 20, bytes_accessed=4 << 20,
-    )(*lists)
+    )(*lists, tables_lower, tables_upper, phase_upper, interp_upper.T)
 
     payload = call(
         middle_kernel, shape(24, 4, 128), [VMEM] * 7, [pltpu.VMEM((4, 8, 128), F32)],

time: 42.1 us -> 41.9 us (level)
  waiting for transfers between devices: 7.21 us -> 8.02 us
  starting transfers between devices: 22.8 us -> 22 us
    ppermute x1, starting transfers between devices: 6.82 us -> 5.87 us  [local(): lax.ppermute(own, CLUS_SAMP, [(i, (i + 1 ^ 1) - 1) for i in range(1, size...]
    ppermute x1, waiting for transfers between devices: 2.56 us -> 3.41 us  [local(): lax.ppermute(own, CLUS_SAMP, [(i, (i + 1 ^ 1) - 1) for i in range(1, size...]
where the time goes in v7:
time: 41.9 us; the launch traced here: 41.6 us
  starting transfers between devices  22 us (53%)
  Pallas kernels  10.9 us (26%)
  waiting for transfers between devices  8.02 us (19%)
  between operations  0.69 us (2%)
    pallas_call x5, Pallas kernels, placed(): run(*(x if spec is VMEM else pltpu.with_memory_space_constraint(x, spec.m...  10.9 us
    all_to_all x1, starting transfers between devices, local(): lax.all_to_all(payload, 'clus_1', split_axis=0, concat_axis=0, tiled=True)  8.47 us
    all_to_all x1, starting transfers between devices, local(): lax.all_to_all(message, LAYER, split_axis=0, concat_axis=0, tiled=True)  7.55 us
    ppermute x1, starting transfers between devices, local(): lax.ppermute(own, CLUS_SAMP, [(i, (i + 1 ^ 1) - 1) for i in range(1, size...  5.87 us
    all_to_all x1, waiting for transfers between devices, local(): lax.all_to_all(message, LAYER, split_axis=0, concat_axis=0, tiled=True)  4.6 us
    ppermute x1, waiting for transfers between devices, local(): lax.ppermute(own, CLUS_SAMP, [(i, (i + 1 ^ 1) - 1) for i in range(1, size...  3.41 us
  transfers between devices with their start and end apart: 4, of which 2 were waited for; matrix products, arithmetic and copies ran while one was open for 0% of the time, Pallas kernels for 16%

profile of v7, /device:TPU:8, one launch (start us, length us, event | category | flops | bytes accessed | tf_op | source)
XLA Modules:
  0.0 41.6 jit_solution(10729391720715446382)
XLA Ops:
  0.6 2.7 %shard_map.184 = (f32[32,8,128]{2,1,0:T(8,128)}, s32[16,256]{1,0:T(8,128)S(1)}, s32[16,256]{1,0:T(8,128)S(1)}, s32[1,256]{1,0:T(1,128)S(1)}, s32[7,32]{1,0:T(8,1...) custom-call(f32[8,2,128]{2,1,0:T(2,128)} %cur_h.3, f32[8,2,2,128,128]{4,3,2,1,0:T(8,128)} %rad_h.1, ...), custom_call_target="tpu_custom_call" | custom-call | flops 4194304 | bytes 3145728 | tf_op jit(solution)/shard_map/pallas_call | solution.py:39
  3.3 7.5 %all-to-all-start = ((f32[32,8,128]{2,1,0:T(8,128)}), f32[32,8,128]{2,1,0:T(8,128)S(1)}, u32[]{:S(2)}, u32[]{:S(2)}) async-start(f32[32,8,128]{2,1,0:T(8,128)} %get-tuple-element.22), calls=%async_computation | async-start | bytes 262144 | tf_op jit(solution)/shard_map/all_to_all | solution.py:334
  10.9 2.0 %shard_map.186 = (f32[8,32,8,128]{3,2,1,0:T(8,128)S(1)}, f32[8,32,8,128]{3,2,1,0:T(8,128)S(1)}, f32[8,4,8,128]{3,2,1,0:T(8,128)S(1)}, f32[8,4,8,128]{3,2,1,0:T(8...) custom-call(s32[16,256]{1,0:T(8,128)S(1)} %get-tuple-element.23.src_low, ...), custom_call_target="tpu_custom_call" | custom-call | flops 1048576 | bytes 4194304 | tf_op jit(solution)/shard_map/pallas_call | solution.py:39
  12.9 4.6 %all-to-all-done = f32[32,8,128]{2,1,0:T(8,128)S(1)} async-done(((f32[32,8,128]{2,1,0:T(8,128)}), f32[32,8,128]{2,1,0:T(8,128)S(1)}, u32[]{:S(2)}, u32[]{:S(2)}) %all-to-all-start) | async-done | bytes 131104 | tf_op jit(solution)/shard_map/all_to_all | solution.py:334
  17.5 1.0 %shard_map.187 = f32[24,4,128]{2,1,0:T(4,128)} custom-call(f32[256,128]{1,0:T(8,128)S(1)} %bitcast.8, bf16[96,768]{1,0:T(8,128)(2,1)S(1)} %get-tuple-element.29.weights, f32[8,32,8,128]{3,2,1,0:T(8,128)S(1)} %get-tuple-element.30.wa, f32[8,32,8,128]{3,2,1,0:T(8,128)S(1)} %get-tuple-element.31.wb, f32[8,4,8,128]{3,2,1,0:T(8,128)S(1)} %get-tuple-element.32.ua, ...), custom_call_target="tpu_custom_call" | custom-call | flops 4194304 | bytes 3145728 | tf_op jit(solution)/shard_map/pallas_call | solution.py:39
  18.4 8.5 %all-to-all-start.1 = ((f32[24,4,128]{2,1,0:T(4,128)}), f32[24,4,128]{2,1,0:T(4,128)S(1)}, u32[]{:S(2)}, u32[]{:S(2)}) async-start(f32[24,4,128]{2,1,0:T(4,128)} %shard_map.187), calls=%async_computation.1 | async-start | bytes 98304 | tf_op jit(solution)/shard_map/all_to_all | solution.py:358
  26.9 5.9 %collective-permute-start.1 = (f32[8,2,128]{2,1,0:T(2,128)}, f32[8,2,128]{2,1,0:T(2,128)S(1)}, u32[]{:S(2)}, u32[]{:S(2)}) collective-permute-start(f32[8,2,128]{2,1,0:T(2,128)} %cur_h.3), channel_id=1, source_target_pairs={{1,2},{2,1},{3,4},{4,3},{5,6},{6,5},{7,8},{8,7},{9,10},{10,9},{11,... | collective-permute-start | bytes 24584 | tf_op jit(solution)/shard_map/ppermute | solution.py:337
  32.8 0.1 collective-permute-start
  32.9 3.4 %collective-permute-done.1.odd = f32[8,2,128]{2,1,0:T(2,128)S(1)} collective-permute-done((f32[8,2,128]{2,1,0:T(2,128)}, f32[8,2,128]{2,1,0:T(2,128)S(1)}, u32[]{:S(2)}, u32[]{:S(2)}) %collective-permute-start.1) | collective-permute-done | bytes 8224 | tf_op jit(solution)/shard_map/ppermute | solution.py:337
  36.3 0.0 collective-permute-done.even
  36.3 4.7 %shard_map.185 = f32[8,2,128]{2,1,0:T(2,128)} custom-call(f32[8,2,128]{2,1,0:T(2,128)} %cur_h.3, f32[8,2,128]{2,1,0:T(2,128)S(1)} %collective-permute-done.even, f32[8,2,128]{2,1,0:T(2,128)S(1)} %collective-permute-done.1.odd, s32[8,8]{1,0:T(8,128)} %neighbours_h.1, s32[8]{0:T(128)} %count_h.1, f32[8,8,2,128,128]{4,3,2,1,0:T(8,128)} %blocks_h.1), custom_call_target="tpu_custom_call" | custom-call | flops 16777216 | bytes 8388608 | tf_op jit(solution)/shard_map/pallas_call | solution.py:39
  41.0 0.0 all-to-all-done.1.got
  41.0 0.6 %shard_map.188 = (f32[1,2,2,256]{3,2,1,0:T(2,128)}, f32[1,2,2,96]{3,2,1,0:T(2,128)}) custom-call(f32[24,4,128]{2,1,0:T(4,128)S(1)} %all-to-all-done.1.got), custom_call_target="tpu_custom_call" | custom-call | flops 131072 | bytes 262144 | tf_op jit(solution)/shard_map/pallas_call | solution.py:39
Async XLA Ops:
  3.3 14.1 %all-to-all-start = ((f32[32,8,128]{2,1,0:T(8,128)}), f32[32,8,128]{2,1,0:T(8,128)S(1)}, u32[]{:S(2)}, u32[]{:S(2)}) async-start(f32[32,8,128]{2,1,0:T(8,128)} %get-tuple-element.22), calls=%async_computation | async-start | bytes 262144 | tf_op jit(solution)/shard_map/all_to_all | solution.py:334
  18.4 22.6 %all-to-all-start.1 = ((f32[24,4,128]{2,1,0:T(4,128)}), f32[24,4,128]{2,1,0:T(4,128)S(1)}, u32[]{:S(2)}, u32[]{:S(2)}) async-start(f32[24,4,128]{2,1,0:T(4,128)} %shard_map.187), calls=%async_computation.1 | async-start | bytes 98304 | tf_op jit(solution)/shard_map/all_to_all | solution.py:358
  26.9 9.4 %collective-permute-start.1 = (f32[8,2,128]{2,1,0:T(2,128)}, f32[8,2,128]{2,1,0:T(2,128)S(1)}, u32[]{:S(2)}, u32[]{:S(2)}) collective-permute-start(f32[8,2,128]{2,1,0:T(2,128)} %cur_h.3), channel_id=1, source_target_pairs={{1,2},{2,1},{3,4},{4,3},{5,6},{6,5},{7,8},{8,7},{9,10},{10,9},{11,... | collective-permute-start | bytes 24584 | tf_op jit(solution)/shard_map/ppermute | solution.py:337
  32.8 3.5 %collective-permute-start = (f32[8,2,128]{2,1,0:T(2,128)}, f32[8,2,128]{2,1,0:T(2,128)S(1)}, u32[]{:S(2)}, u32[]{:S(2)}) collective-permute-start(f32[8,2,128]{2,1,0:T(2,128)} %cur_h.3), channel_id=1, source_target_pairs={{0,1},{1,0},{2,3},{3,2},{4,5},{5,4},{6,7},{7,6},{8,9},{9,8},{10,11... | collective-permute-start | bytes 24584 | tf_op jit(solution)/shard_map/ppermute | solution.py:336
